TPU v7x, 128 devices: a whole 4x4x4 slice. The times are simulated.
128 devices in a mesh: row: 16 (over z_hi, y, core), col: 8 (over x, z_lo).
Axes of the slice: x: 4, y: 4, z: 4 (z_hi: 2, z_lo: 2; z = z_hi * 2 + z_lo), core: 2. Of those that a mesh axis runs over, the one named last changes fastest.
Arguments:
- amplitudes: float32 [16384, 16384], P('row', 'col'), may hold values from -2 to 2
- factors: bfloat16 [16384, 768], P(('row', 'col')), may hold values from -0.0234375 to 0.0234375
- energies: float32 [16384], replicated, may hold values from 0.5 to 2
Outputs:
- amplitude_out: float32 [16384, 16384], P('row', 'col')
All inputs are finite; a program needn't handle non-finite values.
Results may differ from a plain program's by a relative error of at most 0.0074.
Values may be sent and summed in bfloat16 or wider, within the bound.
A program may use at most 128 MiB of HBM per device.

v0:
```python
import math

import jax
import jax.numpy as jnp
from jax import lax
from jax.sharding import PartitionSpec as P

ORDER = 16384
AUX = 768
ITERS = 2


def spread(block, axis, owner):
    block = jnp.where(lax.axis_index(axis) == owner, block, jnp.zeros_like(block))
    return lax.psum(block, axis)


def shards(amplitudes, factors, energies):
    rows_tile, cols_tile = amplitudes.shape
    row_ratio = lax.axis_size("row") // lax.axis_size("col")
    row_index = lax.axis_index("row")
    col_index = lax.axis_index("col")
    row_energy = lax.dynamic_slice_in_dim(energies, row_index * rows_tile, rows_tile)
    col_energy = lax.dynamic_slice_in_dim(energies, col_index * cols_tile, cols_tile)
    denominator = row_energy[:, None] + col_energy[None, :]
    coupling = ORDER / math.sqrt(AUX)
    inv_root = 1.0 / math.sqrt(ORDER)
    factor_rows = lax.all_gather(factors, "col", axis=0, tiled=True)
    collected = []
    for member in range(row_ratio):
        collected.append(spread(factor_rows, "row", col_index * row_ratio + member))
    factor_cols = jnp.concatenate(collected, axis=0)
    amplitude = amplitudes
    for sweep in range(ITERS):
        rounded = amplitude.astype(jnp.bfloat16)
        summed_own = lax.psum_scatter(
            jnp.dot(rounded, factor_cols, preferred_element_type=jnp.float32) * inv_root,
            "col",
            scatter_dimension=0,
            tiled=True,
        )
        dressed_own = (factors.astype(jnp.float32) + summed_own).astype(jnp.bfloat16)
        dressed_rows = lax.all_gather(dressed_own, "col", axis=0, tiled=True)
        summed_cols = lax.psum_scatter(
            lax.dot_general(
                rounded, factor_rows, (((0,), (0,)), ((), ())), preferred_element_type=jnp.float32
            )
            * inv_root,
            "row",
            scatter_dimension=0,
            tiled=True,
        )
        dressed_part = (
            factor_cols.astype(jnp.float32) + lax.all_gather(summed_cols, "row", axis=0, tiled=True)
        ).astype(jnp.bfloat16)
        residual = lax.dot_general(
            dressed_rows, dressed_part, (((1,), (1,)), ((), ())), preferred_element_type=jnp.float32
        )
        amplitude = -coupling * residual / denominator
    return amplitude


def solution(mesh):
    placed = (P("row", "col"), P(("row", "col"), None), P())
    return jax.shard_map(
        shards, mesh=mesh, in_specs=placed, out_specs=P("row", "col"), check_vma=False
    )
```

profile of v0, /device:TPU:1, one launch (start us, length us, event | category | flops | bytes accessed | tf_op | source)
XLA Modules:
  0.0 802.6 jit_solution(10590384602691112871)
XLA Ops:
  6.5 0.7 all-gather.6.cloned.1.call-update
  7.3 46.8 %all-gather.6.cloned.1.call-done = bf16[1024,768]{1,0:T(8,128)(2,1)} async-done(((bf16[128,768]{1,0:T(8,128)(2,1)}), bf16[1024,768]{1,0:T(8,128)(2,1)}) %all-gather.6.cloned.1.call-update) | async-done | bytes 1572880 | tf_op jit(solution)/shard_map/all_gather | solution.py:28
  54.1 3.3 broadcast_select_fusion
  57.4 0.0 reduce-scatter.5.cloned.1.call-start
  57.5 148.8 %all-reduce.3.cloned.1.call-done = (bf16[1024,768]{1,0:T(8,128)(2,1)}, bf16[1024,768]{1,0:T(8,128)(2,1)}) async-done(((bf16[1024,768]{1,0:T(8,128)(2,1)}, bf16[1024,768]{1,0:T(8,128)(2,1)}), (bf16[1024,768]{1,0:T(8,128)(2,1)}, bf16[1024,768]{1,0:T(8,128)(2,1)})) %all-reduce.3.cloned.1.call-update) | async-done | bytes 3145744 | tf_op jit(solution)/shard_map/psum | solution.py:15
  206.3 1.6 constant_dynamic-update-slice_fusion.1
  207.9 0.2 copy-done.2
  208.2 0.1 constant_dynamic-update-slice_fusion
  208.3 1.6 copy-done.3
  209.9 8.5 %multiply_bitcast_fusion = f32[1024,768]{1,0:T(8,128)} fusion(bf16[2048,768]{1,0:T(8,128)(2,1)S(1)} %constant_dynamic-update-slice_fusion, f32[1024,2048]{1,0:T(8,128)} %param.3), kind=kOutput, calls=%fused_computation.9 | convolution fusion | flops 3224109056 | bytes 14680064 | tf_op jit(solution)/shard_map/dot_general | solution.py:37
  218.5 1.3 copy-done.1
  219.8 9.6 %convolution_multiply_fusion.1 = f32[2048,768]{1,0:T(8,128)} fusion(bf16[1024,768]{1,0:T(8,128)(2,1)S(1)} %copy-done.1, f32[1024,2048]{1,0:T(8,128)} %param.3), kind=kOutput, calls=%fused_computation.8 | convolution fusion | flops 3224895488 | bytes 16252928 | tf_op jit(solution)/shard_map/dot_general | solution.py:45
  229.5 60.2 %reduce-scatter.5.cloned.1.call-done = f32[128,768]{1,0:T(8,128)} async-done(((f32[1024,768]{1,0:T(8,128)}), f32[128,768]{1,0:T(8,128)}) %reduce-scatter.5.cloned.1.call-update) | async-done | bytes 393232 | tf_op jit(solution)/shard_map/reduce_scatter | solution.py:36
  289.7 1.7 fusion.10
  291.5 92.5 %reduce-scatter.7.cloned.1.call-done = f32[128,768]{1,0:T(8,128)} async-done(((f32[2048,768]{1,0:T(8,128)}), f32[128,768]{1,0:T(8,128)}) %reduce-scatter.7.cloned.1.call-update) | async-done | bytes 393232 | tf_op jit(solution)/shard_map/reduce_scatter | solution.py:44
  384.0 0.2 reduce-scatter.9.cloned.1.call-start
  384.2 0.7 dynamic_slice.6
  384.9 0.7 dynamic_slice.7
  385.6 41.9 %all-gather.8.cloned.1.call-done = bf16[1024,768]{1,0:T(8,128)(2,1)} async-done(((bf16[128,768]{1,0:T(8,128)(2,1)}), bf16[1024,768]{1,0:T(8,128)(2,1)}) %all-gather.8.cloned.1.call-update) | async-done | bytes 1572880 | tf_op jit(solution)/shard_map/all_gather | solution.py:43
  427.5 68.1 %all-gather.10.cloned.1.call-done = f32[2048,768]{1,0:T(8,128)} async-done(((f32[128,768]{1,0:T(8,128)}), f32[2048,768]{1,0:T(8,128)}) %all-gather.10.cloned.1.call-update) | async-done | bytes 6291472 | tf_op jit(solution)/shard_map/all_gather | solution.py:54
  495.6 7.8 fusion
  503.4 2.1 copy-done.5
  505.5 5.1 convolution_multiply_fusion.2
  510.6 0.0 reduce-scatter.11.cloned.1.call-start
  510.7 8.4 %convolution_multiply_fusion = f32[2048,768]{1,0:T(8,128)} fusion(bf16[1024,2048]{1,0:T(8,128)(2,1)} %copy-done.5, bf16[1024,768]{1,0:T(8,128)(2,1)S(1)} %copy-done.1), kind=kOutput, calls=%fused_computation.7 | convolution fusion | flops 3222798336 | bytes 12058624 | tf_op jit(solution)/shard_map/dot_general | solution.py:45
  519.2 59.5 %reduce-scatter.9.cloned.1.call-done = f32[128,768]{1,0:T(8,128)} async-done(((f32[1024,768]{1,0:T(8,128)}), f32[128,768]{1,0:T(8,128)}) %reduce-scatter.9.cloned.1.call-update) | async-done | bytes 393232 | tf_op jit(solution)/shard_map/reduce_scatter | solution.py:36
  578.7 1.7 fusion.11
  580.4 0.3 all-gather.14.cloned.1.call-start
  580.7 92.2 %reduce-scatter.11.cloned.1.call-done = f32[128,768]{1,0:T(8,128)} async-done(((f32[2048,768]{1,0:T(8,128)}), f32[128,768]{1,0:T(8,128)}) %reduce-scatter.11.cloned.1.call-update) | async-done | bytes 393232 | tf_op jit(solution)/shard_map/reduce_scatter | solution.py:44
  672.9 43.6 %all-gather.12.cloned.1.call-done = bf16[1024,768]{1,0:T(8,128)(2,1)} async-done(((bf16[128,768]{1,0:T(8,128)(2,1)}), bf16[1024,768]{1,0:T(8,128)(2,1)}) %all-gather.12.cloned.1.call-update) | async-done | bytes 1572880 | tf_op jit(solution)/shard_map/all_gather | solution.py:43
  716.5 68.1 %all-gather.14.cloned.1.call-done = f32[2048,768]{1,0:T(8,128)} async-done(((f32[128,768]{1,0:T(8,128)}), f32[2048,768]{1,0:T(8,128)}) %all-gather.14.cloned.1.call-update) | async-done | bytes 6291472 | tf_op jit(solution)/shard_map/all_gather | solution.py:54
  784.7 11.1 %add_divide_fusion = f32[1024,2048]{1,0:T(8,128)} fusion(bf16[1024,768]{1,0:T(8,128)(2,1)} %all-gather.12.cloned.1.call-done, f32[2048]{0:T(1024)S(1)} %dynamic_slice.7, f32[1024]{0:T(1024)S(1)} %dynamic_slice.6, f32[2048,768]{1,0:T(8,128)} %all-gather.14.cloned.1.call-done, bf16[2048,768]{1,0:T(8,128)(2,1)} %copy-done.3), kind=kOutput, calls=%fused_computation | convolution fusion | flops 3232235520 | bytes 19410944 | tf_op jit(solution)/shard_map/dot_general | solution.py:56
  (23 shorter events, 0.4 us)
Async XLA Ops:
  6.5 47.6 %all-gather.6.cloned.1.call-start = ((), (), s32[]{:S(2)}) async-start(), calls=%async_computation.4 | async-start | bytes 1769472 | tf_op jit(solution)/shard_map/all_gather | solution.py:28
  7.3 199.1 %all-reduce.3.cloned.1.call-start = ((), (), s32[]{:S(2)}) async-start(), calls=%async_computation.13 | async-start | bytes 6291456 | tf_op jit(solution)/shard_map/psum | solution.py:15
  57.4 232.3 %reduce-scatter.5.cloned.1.call-start = ((), (), s32[]{:S(2)}) async-start(), calls=%async_computation.5 | async-start | bytes 3538944 | tf_op jit(solution)/shard_map/reduce_scatter | solution.py:36
  206.3 1.9 copy-start.2
  208.3 1.6 copy-start.3
  218.4 1.4 copy-start.1
  218.4 165.5 %reduce-scatter.7.cloned.1.call-start = ((), (), s32[]{:S(2)}) async-start(), calls=%async_computation.7 | async-start | bytes 6684672 | tf_op jit(solution)/shard_map/reduce_scatter | solution.py:44
  229.4 60.3 %copy-start = (bf16[128,768]{1,0:T(8,128)(2,1)S(1)}, bf16[128,768]{1,0:T(8,128)(2,1)}, u32[]{:S(2)}) copy-start(bf16[128,768]{1,0:T(8,128)(2,1)} %param.4) | copy-start | bytes 589828
  229.5 198.0 %all-gather.8.cloned.1.call-start = ((), (), s32[]{:S(2)}) async-start(), calls=%async_computation.6 | async-start | bytes 1769472 | tf_op jit(solution)/shard_map/all_gather | solution.py:43
  291.5 204.2 %all-gather.10.cloned.1.call-start = ((), (), s32[]{:S(2)}) async-start(), calls=%async_computation.8 | async-start | bytes 6684672 | tf_op jit(solution)/shard_map/all_gather | solution.py:54
  384.0 194.7 %reduce-scatter.9.cloned.1.call-start = ((), (), s32[]{:S(2)}) async-start(), calls=%async_computation.9 | async-start | bytes 3538944 | tf_op jit(solution)/shard_map/reduce_scatter | solution.py:36
  495.6 9.9 %copy-start.4 = (bf16[2048,768]{1,0:T(8,128)(2,1)S(1)}, bf16[2048,768]{1,0:T(8,128)(2,1)}, u32[]{:S(2)}) copy-start(bf16[2048,768]{1,0:T(8,128)(2,1)} %copy-done.3) | copy-start | bytes 9437188
  503.4 2.1 copy-start.5
  510.6 162.3 %reduce-scatter.11.cloned.1.call-start = ((), (), s32[]{:S(2)}) async-start(), calls=%async_computation.11 | async-start | bytes 6684672 | tf_op jit(solution)/shard_map/reduce_scatter | solution.py:44
  519.1 197.4 %all-gather.12.cloned.1.call-start = ((), (), s32[]{:S(2)}) async-start(), calls=%async_computation.10 | async-start | bytes 1769472 | tf_op jit(solution)/shard_map/all_gather | solution.py:43
  580.4 204.3 %all-gather.14.cloned.1.call-start = ((), (), s32[]{:S(2)}) async-start(), calls=%async_computation.12 | async-start | bytes 6684672 | tf_op jit(solution)/shard_map/all_gather | solution.py:54
Sparse Core Ops, SparseCore 0:
  9.0 45.0 all-gather.5
  57.5 148.7 all-reduce.2
  218.6 71.1 reduce-scatter.4
  293.7 90.1 reduce-scatter.6
  385.5 41.9 all-gather.7
  429.8 65.8 all-gather.9
  510.7 67.9 reduce-scatter.8
  582.8 89.9 reduce-scatter.10
  674.5 41.9 all-gather.11
  718.8 65.8 all-gather.13
where the time goes:
time: 803 us
  waiting for transfers between devices  723 us (90%)
  matrix products  50.4 us (6%)
  between operations  13.6 us (2%)
  local copies, waits for them, and re-layouts  8.41 us (1%)
    reduce_scatter x2, waiting for transfers between devices, shards(): lax.psum_scatter(lax.dot_general(rounded, factor_rows, (((0,), (0,)), (()...  185 us
    psum x1, waiting for transfers between devices, spread(): return lax.psum(block, axis)  149 us
    all_gather x2, waiting for transfers between devices, shards(): lax.all_gather(summed_cols, 'row', axis=0, tiled=True)  136 us
    reduce_scatter x2, waiting for transfers between devices, shards(): lax.psum_scatter(jnp.dot(rounded, factor_cols, preferred_element_type=jnp...  120 us
    all_gather x2, waiting for transfers between devices, shards(): dressed_rows = lax.all_gather(dressed_own, 'col', axis=0, tiled=True)  85.5 us
    all_gather x1, waiting for transfers between devices, shards(): factor_rows = lax.all_gather(factors, 'col', axis=0, tiled=True)  46.8 us
    dot_general x2, matrix products, shards(): lax.dot_general(dressed_rows, dressed_part, (((1,), (1,)), ((), ())), pre...  18.9 us
    dot_general x2, matrix products, shards(): lax.dot_general(rounded, factor_rows, (((0,), (0,)), ((), ())), preferred...  18 us
  transfers between devices with their start and end apart: 10, of which 10 were waited for; matrix products, arithmetic and copies ran while one was open for 3% of the time, Pallas kernels for 0%

commit v1 on v0

v1 whole, which is shorter than its diff:
```python
import functools
import math

import jax
import jax.numpy as jnp
from jax import lax
from jax.experimental import pallas as pl
from jax.experimental.pallas import tpu as pltpu
from jax.sharding import PartitionSpec as P

ORDER = 16384
AUX = 768
COUPLING = ORDER / math.sqrt(AUX)
INV_ROOT = 1.0 / math.sqrt(ORDER)
MESH = pl.DeviceIdType.MESH
BF16, F32 = jnp.bfloat16, jnp.float32

SLOT = 128
HALF = SLOT // 2
NT = (((1,), (1,)), ((), ()))
TN = (((0,), (0,)), ((), ()))


def rows_at(ref, slot, offset=0, size=SLOT):
    return ref.at[pl.ds(pl.multiple_of(slot * SLOT + offset, HALF), size), :]


class Line:
    def __init__(self, p, m, z, core, own, own_z, sp, sp_z, sm, sm_z, so, so_z):
        self.p, self.m, self.z, self.core = p, m, z, core
        self.own, self.own_z = own, own_z
        self.sp, self.sp_z = sp, sp_z
        self.sm, self.sm_z = sm, sm_z
        self.so, self.so_z = so, so_z


class Gather:
    def __init__(self, line, buf, send, recv, base=0, other=None):
        self.line, self.buf, self.send, self.recv = line, buf, send, recv
        self.base, self.other = base, other
        self.started = []

    def copy(self, i, src, dst, target):
        return pltpu.make_async_remote_copy(
            src_ref=src, dst_ref=dst, send_sem=self.send.at[i], recv_sem=self.recv.at[i],
            device_id=target, device_id_type=MESH,
        )

    def push(self, i, slot, target, offset=0, size=SLOT, src=None):
        dst = rows_at(self.buf, self.base + slot, offset, size)
        c = self.copy(i, dst if src is None else src, dst, target)
        c.start()
        self.started.append(c)

    def arrived(self, i, slot, source, offset=0, size=SLOT):
        dst = rows_at(self.buf, self.base + slot, offset, size)
        self.copy(i, dst, dst, source).wait_recv()

    def to_core(self, i, slot):
        if self.other is not None:
            self.push(9 + i, slot, self.line.core)

    def start(self, src=None):
        ln = self.line
        self.push(0, ln.own, ln.p, src=src)
        self.push(1, ln.own, ln.m, src=src)
        self.push(2, ln.own, ln.z, src=src)
        self.to_core(0, ln.own)

    def pair(self):
        ln = self.line
        self.arrived(2, ln.own_z, ln.z)
        self.push(3, ln.own_z, ln.p)
        self.push(4, ln.own_z, ln.m)
        self.to_core(1, ln.own_z)

    def forward(self):
        ln = self.line
        self.arrived(0, ln.sm, ln.m)
        self.push(5, ln.sm, ln.p, 0, HALF)
        self.to_core(2, ln.sm)
        self.arrived(1, ln.sp, ln.p)
        self.push(6, ln.sp, ln.m, HALF, HALF)
        self.to_core(3, ln.sp)

    def forward_pair(self):
        ln = self.line
        self.arrived(3, ln.sm_z, ln.m)
        self.push(7, ln.sm_z, ln.p, 0, HALF)
        self.to_core(4, ln.sm_z)
        self.arrived(4, ln.sp_z, ln.p)
        self.push(8, ln.sp_z, ln.m, HALF, HALF)
        self.to_core(5, ln.sp_z)

    def last(self):
        ln = self.line
        self.arrived(5, ln.so, ln.m, 0, HALF)
        self.arrived(6, ln.so, ln.p, HALF, HALF)
        self.to_core(6, ln.so)
        self.arrived(7, ln.so_z, ln.m, 0, HALF)
        self.arrived(8, ln.so_z, ln.p, HALF, HALF)
        self.to_core(7, ln.so_z)

    def finish(self):
        ln = self.line
        if self.other is not None:
            order = (ln.own, ln.own_z, ln.sm, ln.sp, ln.sm_z, ln.sp_z, ln.so, ln.so_z)
            for i, slot in enumerate(order):
                dst = rows_at(self.buf, self.other + slot)
                self.copy(9 + i, dst, dst, ln.core).wait_recv()
        for c in self.started:
            c.wait_send()
        self.started = []


class Reduce:
    def __init__(self, line, part, out1, out2, outz, in1, in2, inz, send, recv):
        self.line, self.part = line, part
        self.out1, self.out2, self.outz = out1, out2, outz
        self.in1, self.in2, self.inz = in1, in2, inz
        self.send, self.recv = send, recv
        self.started = []

    def copy(self, i, src, dst, target):
        return pltpu.make_async_remote_copy(
            src_ref=src, dst_ref=dst, send_sem=self.send.at[i], recv_sem=self.recv.at[i],
            device_id=target, device_id_type=MESH,
        )

    def go(self, i, src, dst, target):
        c = self.copy(i, src, dst, target)
        c.start()
        self.started.append(c)

    def get(self, slot, offset, size=HALF):
        return rows_at(self.part, slot, offset, size)[...]

    def opposite(self):
        ln = self.line
        for d, (off, target) in enumerate(((0, ln.p), (HALF, ln.m))):
            self.out1[d, 0:HALF, :] = self.get(ln.so, off).astype(BF16)
            self.out1[d, HALF:SLOT, :] = self.get(ln.so_z, off).astype(BF16)
            self.go(d, self.out1.at[d], self.in1.at[d], target)

    def direct(self, d):
        ln = self.line
        slots, off, target = ((ln.sp, ln.sp_z), HALF, ln.p) if d == 0 else ((ln.sm, ln.sm_z), 0, ln.m)
        self.out2[d, 0, 0:HALF, :] = self.get(slots[0], off).astype(BF16)
        self.out2[d, 0, HALF:SLOT, :] = self.get(slots[1], off).astype(BF16)
        self.go(2 + d, self.out2.at[d, 0], self.in2.at[d, 0], target)

    def dependent(self):
        ln = self.line
        for d in range(2):
            slots, off, target, source = (
                ((ln.sp, ln.sp_z), 0, ln.p, ln.m) if d == 0 else ((ln.sm, ln.sm_z), HALF, ln.m, ln.p)
            )
            self.copy(d, self.in1.at[d], self.in1.at[d], source).wait_recv()
            for h in range(2):
                rows = slice(h * HALF, (h + 1) * HALF)
                total = self.get(slots[h], off) + self.in1[d, rows, :].astype(F32)
                self.out2[d, 1, rows, :] = total.astype(BF16)
            self.go(4 + d, self.out2.at[d, 1], self.in2.at[d, 1], target)

    def summed(self, slot, which):
        rows = slice(which * HALF, (which + 1) * HALF)
        first = self.get(slot, 0) + self.in2[0, 1, rows, :].astype(F32) + self.in2[1, 0, rows, :].astype(F32)
        second = self.get(slot, HALF) + self.in2[0, 0, rows, :].astype(F32) + self.in2[1, 1, rows, :].astype(F32)
        return first, second

    def pair(self):
        ln = self.line
        for d, source in ((0, ln.m), (1, ln.p)):
            self.copy(2 + d, self.in2.at[d, 0], self.in2.at[d, 0], source).wait_recv()
            self.copy(4 + d, self.in2.at[d, 1], self.in2.at[d, 1], source).wait_recv()
        first, second = self.summed(ln.own_z, 1)
        self.outz[0:HALF, :] = first.astype(BF16)
        self.outz[HALF:SLOT, :] = second.astype(BF16)
        self.go(6, self.outz, self.inz, ln.z)

    def dress(self, factors, out):
        ln = self.line
        self.copy(6, self.inz, self.inz, ln.z).wait_recv()
        first, second = self.summed(ln.own, 0)
        for off, total in ((0, first), (HALF, second)):
            rows = pl.ds(off, HALF)
            total = total + self.inz[rows, :].astype(F32)
            out.at[rows, :][...] = (factors.at[rows, :][...].astype(F32) + total).astype(BF16)

    def finish(self):
        for c in self.started:
            c.wait_send()
        self.started = []


def cycle(
    amp, own, energy, dr1, dc1,
    a, stage, fr, fc, dr0, dc0, part_r, part_c, core_out, core_in,
    x1o, x2o, xzo, x1i, x2i, xzi,
    y1o, y2o, yzo, y1i, y2i, yzi,
    e_row, e_col,
    amp_sem, t_sem, agx_s, agx_r, agy_s, agy_r, rsx_s, rsx_r, rsy_s, rsy_r, co_s, co_r,
):
    row, col = lax.axis_index("row"), lax.axis_index("col")
    core, chip_row = lax.rem(row, 2), row // 2
    hi, y = chip_row // 4, lax.rem(chip_row, 4)
    x, lo = col // 2, lax.rem(col, 2)

    def at(r, c):
        return {"row": r, "col": c}

    def x_slot(step, flip):
        return lax.rem(x + step, 4) * 2 + (1 - lo if flip else lo)

    def y_slot(step, flip):
        return (1 - hi if flip else hi) * 4 + lax.rem(y + step, 4)

    def dev_x(step, flip):
        return at(row, x_slot(step, flip))

    def dev_y(step, flip):
        return at(y_slot(step, flip) * 2 + core, col)

    partner = at(chip_row * 2 + 1 - core, col)
    line_x = Line(
        dev_x(1, False), dev_x(3, False), dev_x(0, True), None,
        x_slot(0, False), x_slot(0, True), x_slot(1, False), x_slot(1, True),
        x_slot(3, False), x_slot(3, True), x_slot(2, False), x_slot(2, True),
    )
    line_y = Line(
        dev_y(1, False), dev_y(3, False), dev_y(0, True), partner,
        y_slot(0, False), y_slot(0, True), y_slot(1, False), y_slot(1, True),
        y_slot(3, False), y_slot(3, True), y_slot(2, False), y_slot(2, True),
    )
    mirror = at(col * 2 + core, chip_row)
    off_diagonal = chip_row != col

    def amp_copy(i):
        return pltpu.make_async_copy(amp.at[pl.ds(i * 256, 256), :], stage.at[i % 2], amp_sem.at[i % 2])

    amp_copy(0).start()
    amp_copy(1).start()

    barrier = pltpu.get_barrier_semaphore()
    for ln in (line_x, line_y):
        for device in (ln.p, ln.m, ln.z):
            pl.semaphore_signal(barrier, inc=1, device_id=device, device_id_type=MESH)
    pl.semaphore_signal(barrier, inc=1, device_id=partner, device_id_type=MESH)

    @pl.when(off_diagonal)
    def _():
        pl.semaphore_signal(barrier, inc=1, device_id=mirror, device_id_type=MESH)

    for j in range(8):
        v = energy[pl.ds(row * 8 + j, 1), :]
        e_row[j * 128 : (j + 1) * 128, :] = jnp.broadcast_to(v, (128, 128)).T
    for j in range(16):
        e_col[:, j * 128 : (j + 1) * 128] = energy[pl.ds(col * 16 + j, 1), :]

    @pl.when(off_diagonal)
    def _():
        pl.semaphore_wait(barrier, 8)

    @pl.when(jnp.logical_not(off_diagonal))
    def _():
        pl.semaphore_wait(barrier, 7)

    half_c, other_c = core * 8, (1 - core) * 8
    gx = Gather(line_x, fr, agx_s.at[0], agx_r.at[0])
    gy = Gather(line_y, fc, agy_s.at[0], agy_r.at[0], half_c, other_c)
    gx.start(src=own)
    mine_c = rows_at(fc, half_c + chip_row)
    theirs = rows_at(fc, half_c + col)
    t_send = pltpu.make_async_remote_copy(
        src_ref=own, dst_ref=theirs, send_sem=t_sem.at[0], recv_sem=t_sem.at[1],
        device_id=mirror, device_id_type=MESH,
    )

    @pl.when(off_diagonal)
    def _():
        t_send.start()

    rows_at(fr, line_x.own)[...] = own[...]

    @pl.when(jnp.logical_not(off_diagonal))
    def _():
        mine_c[...] = own[...]

    for i in range(4):
        amp_copy(i).wait()
        a[i * 256 : (i + 1) * 256, :] = stage[i % 2].astype(BF16)
        if i + 2 < 4:
            amp_copy(i + 2).start()

    gx.pair()
    gx.forward()
    gx.forward_pair()

    @pl.when(off_diagonal)
    def _():
        pltpu.make_async_remote_copy(
            src_ref=own, dst_ref=mine_c, send_sem=t_sem.at[0], recv_sem=t_sem.at[1],
            device_id=mirror, device_id_type=MESH,
        ).wait_recv()

    gy.start()
    gx.last()

    def mm_rows(s):
        at_rows = pl.ds(pl.multiple_of((s // 2) * 256, 256), 256)
        part_r[at_rows, :] = (
            jnp.dot(a[at_rows, :], fc[...], preferred_element_type=F32) * INV_ROOT
        )

    def mm_cols(half, s, s_z):
        lhs = [
            a[:, pl.ds(pl.multiple_of((half + i) * SLOT, SLOT), SLOT)] for i in (s, s_z)
        ]
        lhs = jnp.concatenate(lhs, axis=1)
        return lax.dot_general(lhs, fr[...], TN, preferred_element_type=F32) * INV_ROOT

    pairs_y = (
        (line_y.so, line_y.so_z), (line_y.sp, line_y.sp_z), (line_y.sm, line_y.sm_z), (line_y.own, line_y.own_z),
    )

    for it in range(2):
        rsx = Reduce(
            line_x, part_r, x1o, x2o, xzo, x1i.at[it], x2i.at[it], xzi.at[it], rsx_s.at[it], rsx_r.at[it]
        )
        rsy = Reduce(
            line_y, part_c, y1o, y2o, yzo, y1i.at[it], y2i.at[it], yzi.at[it], rsy_s.at[it], rsy_r.at[it]
        )

        def core_copy(i):
            return pltpu.make_async_remote_copy(
                src_ref=core_out.at[i], dst_ref=core_in.at[it, i],
                send_sem=co_s.at[it, i], recv_sem=co_r.at[it, i],
                device_id=partner, device_id_type=MESH,
            )

        def other_half(i):
            core_out[i] = mm_cols(other_c, *pairs_y[i]).astype(BF16)
            core_copy(i).start()

        def own_half(i):
            value = mm_cols(half_c, *pairs_y[i])
            core_copy(i).wait_recv()
            value = value + core_in[it, i].astype(F32)
            rows_at(part_c, pairs_y[i][0])[...] = value[:SLOT]
            rows_at(part_c, pairs_y[i][1])[...] = value[SLOT:]

        if it == 0:
            other_half(0)
            other_half(1)
            gy.forward()
            gy.pair()
            other_half(2)
            other_half(3)
            own_half(0)
            own_half(1)
            gy.forward_pair()
            own_half(2)
            own_half(3)
            gy.last()
            rsy.opposite()
            rsy.direct(0)
            rsy.direct(1)
            gy.finish()
            mm_rows(line_x.so)
            rsx.opposite()
            mm_rows(line_x.sp)
            rsx.direct(0)
            mm_rows(line_x.sm)
            rsx.direct(1)
            rsy.dependent()
            mm_rows(line_x.own)
            rsx.dependent()
        else:
            for i in range(4):
                other_half(i)
            mm_rows(line_x.so)
            rsx.opposite()
            own_half(0)
            rsy.opposite()
            mm_rows(line_x.sp)
            rsx.direct(0)
            mm_rows(line_x.sm)
            rsx.direct(1)
            own_half(1)
            rsy.direct(0)
            own_half(2)
            rsy.direct(1)
            rsx.dependent()
            mm_rows(line_x.own)
            rsy.dependent()
            own_half(3)
        rsy.pair()
        rsx.pair()

        dr, dc = (dr0, dc0) if it == 0 else (dr1, dc1)
        hx = Gather(line_x, dr, agx_s.at[it + 1], agx_r.at[it + 1])
        hy = Gather(line_y, dc, agy_s.at[it + 1], agy_r.at[it + 1], half_c, other_c)
        rsy.dress(mine_c, rows_at(dc, half_c + chip_row))
        hy.start()
        rsx.dress(own, rows_at(dr, line_x.own))
        hx.start()
        hx.pair()
        hy.forward()
        hx.forward()
        hy.pair()
        hx.forward_pair()
        hy.forward_pair()
        hx.last()
        hy.last()
        for i in range(4):
            core_copy(i).wait_send()
        rsx.finish()
        rsy.finish()
        hx.finish()
        hy.finish()

        if it == 0:

            @pl.loop(0, 4)
            def _(i):
                at_rows = pl.ds(pl.multiple_of(i * 256, 256), 256)
                for j in range(4):
                    cols = slice(j * 512, (j + 1) * 512)
                    residual = lax.dot_general(
                        dr0[at_rows, :], dc0[cols, :], NT, preferred_element_type=F32
                    )
                    den = jnp.concatenate([e_row[at_rows, :]] * 4, axis=1) + e_col[:, cols]
                    a[at_rows, cols] = (-COUPLING * residual / den).astype(BF16)

    gx.finish()

    @pl.when(off_diagonal)
    def _():
        t_send.wait_send()


def dma(*shape):
    return pltpu.SemaphoreType.DMA(shape)


def shards(amplitudes, factors, energies):
    row_tile, col_tile = amplitudes.shape
    vmem = pl.BlockSpec(memory_space=pltpu.VMEM)

    def line_buffers():
        return [
            pltpu.VMEM((2, SLOT, AUX), BF16),
            pltpu.VMEM((2, 2, SLOT, AUX), BF16),
            pltpu.VMEM((SLOT, AUX), BF16),
            pltpu.VMEM((2, 2, SLOT, AUX), BF16),
            pltpu.VMEM((2, 2, 2, SLOT, AUX), BF16),
            pltpu.VMEM((2, SLOT, AUX), BF16),
        ]

    dr, dc = pl.pallas_call(
        cycle,
        out_shape=(
            jax.ShapeDtypeStruct((row_tile, AUX), BF16),
            jax.ShapeDtypeStruct((col_tile, AUX), BF16),
        ),
        in_specs=[pl.BlockSpec(memory_space=pl.ANY), vmem, vmem],
        out_specs=(vmem, vmem),
        scratch_shapes=[
            pltpu.VMEM((row_tile, col_tile), BF16),
            pltpu.VMEM((2, 256, col_tile), F32),
            pltpu.VMEM((row_tile, AUX), BF16),
            pltpu.VMEM((col_tile, AUX), BF16),
            pltpu.VMEM((row_tile, AUX), BF16),
            pltpu.VMEM((col_tile, AUX), BF16),
            pltpu.VMEM((row_tile, AUX), F32),
            pltpu.VMEM((row_tile, AUX), F32),
            pltpu.VMEM((4, 256, AUX), BF16),
            pltpu.VMEM((2, 4, 256, AUX), BF16),
            *line_buffers(),
            *line_buffers(),
            pltpu.VMEM((row_tile, 128), F32),
            pltpu.VMEM((1, col_tile), F32),
            dma(2), dma(2),
            dma(3, 9), dma(3, 9), dma(3, 17), dma(3, 17),
            dma(2, 7), dma(2, 7), dma(2, 7), dma(2, 7),
            dma(2, 4), dma(2, 4),
        ],
        compiler_params=pltpu.CompilerParams(
            collective_id=0, has_side_effects=True, vmem_limit_bytes=60 * 1024 * 1024
        ),
        name="cycle",
    )(amplitudes, factors, energies.reshape(128, 128))

    row_energy = lax.dynamic_slice_in_dim(energies, lax.axis_index("row") * row_tile, row_tile)
    col_energy = lax.dynamic_slice_in_dim(energies, lax.axis_index("col") * col_tile, col_tile)
    residual = lax.dot_general(dr, dc, NT, preferred_element_type=F32)
    return -COUPLING * residual / (row_energy[:, None] + col_energy[None, :])


def solution(mesh):
    placed = (P("row", "col"), P(("row", "col"), None), P())
    return jax.shard_map(
        shards, mesh=mesh, in_specs=placed, out_specs=P("row", "col"), check_vma=False
    )
```

time: 803 us -> 167 us (0.21)
  waiting for transfers between devices: 723 us -> 0 us
  Pallas kernels: 0 us -> 156 us
  matrix products: 50.4 us -> 9.23 us
  between operations: 13.6 us -> 0.01 us
    reduce_scatter x4 -> x0, waiting for transfers between devices: 304 us -> none  [the longest x2 185 us: shards(): lax.psum_scatter(lax.dot_general(rounded, factor_rows, (((0,), (0,)), (()...]
    all_gather x5 -> x0, waiting for transfers between devices: 269 us -> none  [the longest x2 136 us: shards(): lax.all_gather(summed_cols, 'row', axis=0, tiled=True)]
    pallas_call x0 -> x1, Pallas kernels: none -> 156 us  [shards(): pl.pallas_call(cycle, out_shape=(jax.ShapeDtypeStruct((row_tile, AUX), BF...]
    psum x1 -> x0, waiting for transfers between devices: 149 us -> none  [spread(): return lax.psum(block, axis)]
    dot_general x6 -> x1, matrix products: 50.4 us -> 9.23 us  [shards(): residual = lax.dot_general(dr, dc, NT, preferred_element_type=F32)]
  transfers between devices with their start and end apart: 10 -> 0, of which waited for: 10 -> 0; matrix products, arithmetic and copies ran while one was open for 3% -> 0% of each run, Pallas kernels for 0% -> 0%
where the time goes in v1:
time: 167 us
  Pallas kernels  156 us (93%)
  matrix products  9.23 us (6%)
    pallas_call x1, Pallas kernels, shards(): pl.pallas_call(cycle, out_shape=(jax.ShapeDtypeStruct((row_tile, AUX), BF...  156 us
    dot_general x1, matrix products, shards(): residual = lax.dot_general(dr, dc, NT, preferred_element_type=F32)  9.23 us

profile of v1, /device:TPU:1, one launch (start us, length us, event | category | flops | bytes accessed | tf_op | source)
XLA Modules:
  0.0 166.7 jit_solution(13141304733858950600)
XLA Ops:
  0.0 0.7 dynamic_slice.6
  0.7 0.7 dynamic_slice.7
  1.4 156.1 %cycle.1 = (bf16[1024,768]{1,0:T(8,128)(2,1)}, bf16[2048,768]{1,0:T(8,128)(2,1)}) custom-call(f32[1024,2048]{1,0:T(8,128)} %amp.1, bf16[128,768]{1,0:T(8,128)(2,1)} %own.1, f32[128,128]{1,0:T(8,128)} %bitcast.3), custom_call_target="tpu_custom_call" | custom-call | tf_op jit(solution)/shard_map/cycle/pallas_call | solution.py:460
  157.5 9.2 %add_divide_fusion = f32[1024,2048]{1,0:T(8,128)} fusion(bf16[1024,768]{1,0:T(8,128)(2,1)} %get-tuple-element.7, bf16[2048,768]{1,0:T(8,128)(2,1)} %get-tuple-element.8, f32[2048]{0:T(1024)S(1)} %dynamic_slice.7, f32[1024]{0:T(1024)S(1)} %dynamic_slice.6), kind=kOutput, calls=%fused_computation | convolution fusion | flops 3227516928 | bytes 13119488 | tf_op jit(solution)/shard_map/dot_general | solution.py:496

commit v2 on v0

v2 whole, which is shorter than its diff:
```python
import functools
import math

import jax
import jax.numpy as jnp
from jax import lax
from jax.experimental import pallas as pl
from jax.experimental.pallas import tpu as pltpu
from jax.sharding import PartitionSpec as P

ORDER = 16384
AUX = 768
COUPLING = ORDER / math.sqrt(AUX)
INV_ROOT = 1.0 / math.sqrt(ORDER)
MESH = pl.DeviceIdType.MESH
BF16, F32 = jnp.bfloat16, jnp.float32

SLOT = 128
HALF = SLOT // 2
K = AUX // 2
NT = (((1,), (1,)), ((), ()))
TN = (((0,), (0,)), ((), ()))


def part_of(ref, slot, k=None, offset=0, size=SLOT):
    rows = pl.ds(pl.multiple_of(slot * SLOT + offset, HALF), size)
    return ref.at[rows, :] if k is None else ref.at[rows, pl.ds(k * K, K)]


class Line:
    def __init__(self, device, slot, core=None):
        self.p, self.m, self.o, self.z = device(1, 0), device(3, 0), device(2, 0), device(0, 1)
        self.core = core
        self.own, self.own_z = slot(0, 0), slot(0, 1)
        self.sp, self.sp_z = slot(1, 0), slot(1, 1)
        self.sm, self.sm_z = slot(3, 0), slot(3, 1)
        self.so, self.so_z = slot(2, 0), slot(2, 1)


class Exchange:
    def __init__(self, send, recv):
        self.send, self.recv = send, recv
        self.started = []

    def copy(self, i, src, dst, target):
        return pltpu.make_async_remote_copy(
            src_ref=src, dst_ref=dst, send_sem=self.send.at[i], recv_sem=self.recv.at[i],
            device_id=target, device_id_type=MESH,
        )

    def go(self, i, src, dst, target):
        c = self.copy(i, src, dst, target)
        c.start()
        self.started.append(c)

    def got(self, i, dst, source):
        self.copy(i, dst, dst, source).wait_recv()

    def sent(self):
        for c in self.started:
            c.wait_send()
        self.started = []


class Gather(Exchange):
    def __init__(self, line, buf, k, send, recv, base=0, other=None, relay_own=False, relay_pair=False):
        super().__init__(send, recv)
        self.line, self.buf, self.k = line, buf, k
        self.base, self.other = base, other
        self.relay_own, self.relay_pair = relay_own, relay_pair

    def view(self, slot, offset=0, size=SLOT):
        return part_of(self.buf, self.base + slot, self.k, offset, size)

    def push(self, i, slot, target, offset=0, size=SLOT, src=None):
        dst = self.view(slot, offset, size)
        self.go(i, dst if src is None else src, dst, target)

    def arrived(self, i, slot, source, offset=0, size=SLOT):
        self.got(i, self.view(slot, offset, size), source)

    def to_core(self, i, slot):
        if self.other is not None:
            self.push(9 + i, slot, self.line.core)

    def start(self, src=None):
        ln = self.line
        self.push(2, ln.own, ln.z, src=src)
        if not self.relay_own:
            self.push(5, ln.own, ln.o, src=src)
        self.push(0, ln.own, ln.p, src=src)
        self.push(1, ln.own, ln.m, src=src)
        self.to_core(0, ln.own)

    def pair(self):
        ln = self.line
        self.arrived(2, ln.own_z, ln.z)
        if not self.relay_pair:
            self.push(7, ln.own_z, ln.o)
        self.push(3, ln.own_z, ln.p)
        self.push(4, ln.own_z, ln.m)
        self.to_core(1, ln.own_z)

    def near(self):
        ln = self.line
        self.arrived(0, ln.sm, ln.m)
        if self.relay_own:
            self.push(5, ln.sm, ln.p, 0, HALF)
        self.to_core(2, ln.sm)
        self.arrived(1, ln.sp, ln.p)
        if self.relay_own:
            self.push(6, ln.sp, ln.m, HALF, HALF)
        self.to_core(3, ln.sp)

    def near_pair(self):
        ln = self.line
        self.arrived(3, ln.sm_z, ln.m)
        if self.relay_pair:
            self.push(7, ln.sm_z, ln.p, 0, HALF)
        self.to_core(4, ln.sm_z)
        self.arrived(4, ln.sp_z, ln.p)
        if self.relay_pair:
            self.push(8, ln.sp_z, ln.m, HALF, HALF)
        self.to_core(5, ln.sp_z)

    def far(self):
        ln = self.line
        if self.relay_own:
            self.arrived(5, ln.so, ln.m, 0, HALF)
            self.arrived(6, ln.so, ln.p, HALF, HALF)
        else:
            self.arrived(5, ln.so, ln.o)
        self.to_core(6, ln.so)

    def far_pair(self):
        ln = self.line
        if self.relay_pair:
            self.arrived(7, ln.so_z, ln.m, 0, HALF)
            self.arrived(8, ln.so_z, ln.p, HALF, HALF)
        else:
            self.arrived(7, ln.so_z, ln.o)
        self.to_core(7, ln.so_z)

    def from_core(self):
        ln = self.line
        order = (ln.own, ln.own_z, ln.sm, ln.sp, ln.sm_z, ln.sp_z, ln.so, ln.so_z)
        for i, slot in enumerate(order):
            self.got(9 + i, part_of(self.buf, self.other + slot, self.k), ln.core)


class Reduce(Exchange):
    def __init__(self, line, part, out, outz, into, inz, send, recv):
        super().__init__(send, recv)
        self.line, self.part = line, part
        self.out, self.outz, self.into, self.inz = out, outz, into, inz

    def give(self, d):
        ln = self.line
        slots, target = (
            ((ln.sp_z, ln.sp), ln.p), ((ln.sm_z, ln.sm), ln.m), ((ln.so_z, ln.so), ln.o),
        )[d]
        for h in range(2):
            self.out[d, h] = part_of(self.part, slots[h])[...].astype(BF16)
            self.go(2 * d + h, self.out.at[d, h], self.into.at[d, h], target)

    def collect(self, h):
        ln = self.line
        for d, source in ((0, ln.m), (1, ln.p), (2, ln.o)):
            self.got(2 * d + h, self.into.at[d, h], source)
        total = part_of(self.part, ln.own if h else ln.own_z)[...]
        for d in range(3):
            total = total + self.into[d, h].astype(F32)
        return total

    def pair(self):
        self.outz[...] = self.collect(0).astype(BF16)
        self.go(6, self.outz, self.inz, self.line.z)

    def total(self):
        total = self.collect(1)
        self.got(6, self.inz, self.line.z)
        return total + self.inz[...].astype(F32)


def cycle(
    amp, own, energy, dr1, dc1,
    a, stage, fr, fc, own_c, dr0, dc0, part_r, part_c, core_out, core_in,
    x_out, x_outz, x_in, x_inz, y_out, y_outz, y_in, y_inz,
    e_row, e_col,
    amp_sem, turn_s, turn_r, agx_s, agx_r, agy_s, agy_r, rsx_s, rsx_r, rsy_s, rsy_r, co_s, co_r,
):
    row, col = lax.axis_index("row"), lax.axis_index("col")
    core, chip_row = lax.rem(row, 2), row // 2
    hi, y = chip_row // 4, lax.rem(chip_row, 4)
    x, lo = col // 2, lax.rem(col, 2)

    def at(r, c):
        return {"row": r, "col": c}

    def x_slot(step, flip):
        return lax.rem(x + step, 4) * 2 + (1 - lo if flip else lo)

    first_y = lax.rem(x, 2) * 2 + lo
    parity = x // 2 + lo

    def y_slot(step, flip):
        z = 1 - hi if flip else hi
        return lax.rem(x + y + step + 4 - first_y, 4) * 2 + lax.rem(z + parity, 2)

    def dev_x(step, flip):
        return at(row, x_slot(step, flip))

    def dev_y(step, flip):
        z = 1 - hi if flip else hi
        return at((z * 4 + lax.rem(y + step, 4)) * 2 + core, col)

    partner = at(chip_row * 2 + 1 - core, col)
    line_x = Line(dev_x, x_slot)
    line_y = Line(dev_y, y_slot, partner)

    x_to = chip_row // 2
    y_to = lax.rem(y + x + 4 - x_to, 4)
    hi_to = lax.rem(hi + lo + y, 2)
    to_row, to_col = (hi_to * 4 + y_to) * 2 + core, x_to * 2 + lax.rem(y, 2)
    turn_to = at(to_row, to_col)
    turn_from = at(col * 2 + core, line_y.own)
    moves = (to_row - row) * (to_row - row) + (to_col - col) * (to_col - col) != 0
    stays = jnp.logical_not(moves)

    half_c, other_c = core * 8, (1 - core) * 8
    mine_r, mine_c = line_x.own, half_c + line_y.own

    def turn(i, src, dst, device):
        return pltpu.make_async_remote_copy(
            src_ref=src, dst_ref=dst, send_sem=turn_s.at[i], recv_sem=turn_r.at[i],
            device_id=device, device_id_type=MESH,
        )

    def amp_copy(i):
        return pltpu.make_async_copy(amp.at[pl.ds(i * 256, 256), :], stage.at[i % 2], amp_sem.at[i % 2])

    amp_copy(0).start()
    amp_copy(1).start()

    barrier = pltpu.get_barrier_semaphore()

    def greet(device):
        pl.semaphore_signal(barrier, inc=1, device_id=device, device_id_type=MESH)

    for ln in (line_x, line_y):
        for device in (ln.p, ln.m, ln.o, ln.z):
            greet(device)
    greet(partner)

    @pl.when(moves)
    def _():
        greet(turn_to)
        greet(turn_from)

    for j in range(8):
        v = energy[pl.ds(row * 8 + j, 1), :]
        e_row[j * 128 : (j + 1) * 128, :] = jnp.broadcast_to(v, (128, 128)).T
    for j in range(16):
        e_col[:, j * 128 : (j + 1) * 128] = energy[pl.ds(col * 16 + j, 1), :]

    @pl.when(moves)
    def _():
        pl.semaphore_wait(barrier, 11)

    @pl.when(stays)
    def _():
        pl.semaphore_wait(barrier, 9)

    gx = Gather(line_x, fr, None, agx_s.at[0], agx_r.at[0])
    gy = Gather(line_y, fc, None, agy_s.at[0], agy_r.at[0], half_c, other_c)
    own0, own1 = own.at[:, pl.ds(0, K)], own.at[:, pl.ds(K, K)]
    turn_f0 = turn(0, own0, part_of(fc, half_c + col), turn_to)
    turn_f1 = turn(1, own1, own_c, turn_to)

    @pl.when(moves)
    def _():
        turn_f0.start()

    gx.start(src=own1)

    @pl.when(moves)
    def _():
        turn_f1.start()

    part_of(fr, mine_r)[...] = own1[...]

    @pl.when(stays)
    def _():
        part_of(fc, mine_c)[...] = own0[...]
        own_c[...] = own1[...]

    for i in range(4):
        amp_copy(i).wait()
        a[i * 256 : (i + 1) * 256, :] = stage[i % 2].astype(BF16)
        if i + 2 < 4:
            amp_copy(i + 2).start()

    gx.pair()

    @pl.when(moves)
    def _():
        turn(0, own0, part_of(fc, mine_c), turn_from).wait_recv()

    gy.start()
    gx.near()
    gx.far()
    gy.pair()
    gx.near_pair()
    gx.far_pair()

    def mm_rows(s):
        at_rows = pl.ds(pl.multiple_of((s // 2) * 256, 256), 256)
        part_r[at_rows, :] = jnp.dot(a[at_rows, :], fc[...], preferred_element_type=F32) * INV_ROOT

    def mm_cols(half, s, s_z):
        lhs = [a[:, pl.ds(pl.multiple_of((half + i) * SLOT, SLOT), SLOT)] for i in (s, s_z)]
        lhs = jnp.concatenate(lhs, axis=1)
        return lax.dot_general(lhs, fr[...], TN, preferred_element_type=F32) * INV_ROOT

    pairs_y = (
        (line_y.so, line_y.so_z), (line_y.sp, line_y.sp_z), (line_y.sm, line_y.sm_z), (line_y.own, line_y.own_z),
    )

    for it in range(2):
        dr, dc = (dr0, dc0) if it == 0 else (dr1, dc1)
        rsx = Reduce(line_x, part_r, x_out, x_outz, x_in.at[it], x_inz.at[it], rsx_s.at[it], rsx_r.at[it])
        rsy = Reduce(line_y, part_c, y_out, y_outz, y_in.at[it], y_inz.at[it], rsy_s.at[it], rsy_r.at[it])

        def core_copy(i):
            return pltpu.make_async_remote_copy(
                src_ref=core_out.at[i], dst_ref=core_in.at[it, i],
                send_sem=co_s.at[it, i], recv_sem=co_r.at[it, i],
                device_id=partner, device_id_type=MESH,
            )

        def other_half(i):
            core_out[i] = mm_cols(other_c, *pairs_y[i]).astype(BF16)
            core_copy(i).start()

        def own_half(i):
            value = mm_cols(half_c, *pairs_y[i])
            core_copy(i).wait_recv()
            value = value + core_in[it, i].astype(F32)
            part_of(part_c, pairs_y[i][0])[...] = value[:SLOT]
            part_of(part_c, pairs_y[i][1])[...] = value[SLOT:]

        if it == 0:
            other_half(0)
            other_half(1)
            gy.near()
            gy.far()
            other_half(2)
            other_half(3)
            own_half(0)
            rsy.give(2)
            own_half(1)
            rsy.give(0)
            gy.near_pair()
            gy.far_pair()
            own_half(2)
            rsy.give(1)
            own_half(3)
            gy.from_core()
            mm_rows(line_x.so)
            rsx.give(2)
            mm_rows(line_x.sp)
            rsx.give(0)
            mm_rows(line_x.sm)
            rsx.give(1)
            mm_rows(line_x.own)
        else:
            mm_rows(line_x.so)
            rsx.give(2)
            for i in range(4):
                other_half(i)
            own_half(0)
            rsy.give(2)
            own_half(1)
            rsy.give(0)
            own_half(2)
            rsy.give(1)
            mm_rows(line_x.sp)
            rsx.give(0)
            mm_rows(line_x.sm)
            rsx.give(1)
            own_half(3)
            mm_rows(line_x.own)
        rsy.pair()
        rsx.pair()

        hx = [Gather(line_x, dr, k, agx_s.at[1 + 2 * it + k], agx_r.at[1 + 2 * it + k]) for k in range(2)]
        hy = [
            Gather(line_y, dc, k, agy_s.at[1 + 2 * it + k], agy_r.at[1 + 2 * it + k], half_c, other_c)
            for k in range(2)
        ]
        r0, r1 = part_of(dr, mine_r, 0), part_of(dr, mine_r, 1)
        c0, c1 = part_of(dc, mine_c, 0), part_of(dc, mine_c, 1)
        turn_c = turn(2 + 2 * it, c1, part_of(dr, line_y.own, 1), turn_from)
        turn_r_ = turn(3 + 2 * it, r0, part_of(dc, half_c + col, 0), turn_to)

        if it == 0:

            @pl.when(moves)
            def _():
                turn(1, own1, own_c, turn_from).wait_recv()

        c1[...] = (own_c[...].astype(F32) + rsy.total()).astype(BF16)

        @pl.when(moves)
        def _():
            turn_c.start()

        hy[1].start()
        r0[...] = (own0[...].astype(F32) + rsx.total()).astype(BF16)

        @pl.when(moves)
        def _():
            turn_r_.start()

        hx[0].start()

        @pl.when(stays)
        def _():
            r1[...] = c1[...]
            c0[...] = r0[...]

        hy[1].pair()
        hx[0].pair()

        @pl.when(moves)
        def _():
            turn(2 + 2 * it, r1, r1, turn_to).wait_recv()

        hx[1].start()

        @pl.when(moves)
        def _():
            turn(3 + 2 * it, c0, c0, turn_from).wait_recv()

        hy[0].start()
        hy[1].near()
        hx[0].near()
        hy[1].far()
        hx[0].far()
        hy[1].near_pair()
        hx[0].near_pair()
        hx[1].pair()
        hy[0].pair()
        hy[1].far_pair()
        hx[0].far_pair()
        hy[0].near()
        hx[1].near()
        hy[0].far()
        hx[1].far()
        hy[0].near_pair()
        hx[1].near_pair()
        hy[0].far_pair()
        hx[1].far_pair()
        hy[1].from_core()
        hy[0].from_core()

        if it == 0:

            @pl.loop(0, 4)
            def _(i):
                at_rows = pl.ds(pl.multiple_of(i * 256, 256), 256)
                for j in range(4):
                    cols = slice(j * 512, (j + 1) * 512)
                    residual = lax.dot_general(
                        dr0[at_rows, :], dc0[cols, :], NT, preferred_element_type=F32
                    )
                    den = jnp.concatenate([e_row[at_rows, :]] * 4, axis=1) + e_col[:, cols]
                    a[at_rows, cols] = (-COUPLING * residual / den).astype(BF16)

        for i in range(4):
            core_copy(i).wait_send()
        for exchange in (rsx, rsy, *hx, *hy):
            exchange.sent()

        @pl.when(moves)
        def _():
            turn_c.wait_send()
            turn_r_.wait_send()

    gx.sent()
    gy.sent()

    @pl.when(moves)
    def _():
        turn_f0.wait_send()
        turn_f1.wait_send()


def dma(*shape):
    return pltpu.SemaphoreType.DMA(shape)


def shards(amplitudes, factors, energies):
    row_tile, col_tile = amplitudes.shape
    vmem = pl.BlockSpec(memory_space=pltpu.VMEM)

    def line_buffers():
        return [
            pltpu.VMEM((3, 2, SLOT, K), BF16),
            pltpu.VMEM((SLOT, K), BF16),
            pltpu.VMEM((2, 3, 2, SLOT, K), BF16),
            pltpu.VMEM((2, SLOT, K), BF16),
        ]

    dr, dc = pl.pallas_call(
        cycle,
        out_shape=(
            jax.ShapeDtypeStruct((row_tile, AUX), BF16),
            jax.ShapeDtypeStruct((col_tile, AUX), BF16),
        ),
        in_specs=[pl.BlockSpec(memory_space=pl.ANY), vmem, vmem],
        out_specs=(vmem, vmem),
        scratch_shapes=[
            pltpu.VMEM((row_tile, col_tile), BF16),
            pltpu.VMEM((2, 256, col_tile), F32),
            pltpu.VMEM((row_tile, K), BF16),
            pltpu.VMEM((col_tile, K), BF16),
            pltpu.VMEM((SLOT, K), BF16),
            pltpu.VMEM((row_tile, AUX), BF16),
            pltpu.VMEM((col_tile, AUX), BF16),
            pltpu.VMEM((row_tile, K), F32),
            pltpu.VMEM((row_tile, K), F32),
            pltpu.VMEM((4, 256, K), BF16),
            pltpu.VMEM((2, 4, 256, K), BF16),
            *line_buffers(),
            *line_buffers(),
            pltpu.VMEM((row_tile, 128), F32),
            pltpu.VMEM((1, col_tile), F32),
            dma(2), dma(6), dma(6),
            dma(5, 9), dma(5, 9), dma(5, 17), dma(5, 17),
            dma(2, 7), dma(2, 7), dma(2, 7), dma(2, 7),
            dma(2, 4), dma(2, 4),
        ],
        compiler_params=pltpu.CompilerParams(
            collective_id=0, has_side_effects=True, vmem_limit_bytes=50 * 1024 * 1024
        ),
        name="cycle",
    )(amplitudes, factors, energies.reshape(128, 128))

    row_energy = lax.dynamic_slice_in_dim(energies, lax.axis_index("row") * row_tile, row_tile)
    col_energy = lax.dynamic_slice_in_dim(energies, lax.axis_index("col") * col_tile, col_tile)
    residual = lax.dot_general(dr, dc, NT, preferred_element_type=F32)
    return -COUPLING * residual / (row_energy[:, None] + col_energy[None, :])


def solution(mesh):
    placed = (P("row", "col"), P(("row", "col"), None), P())
    return jax.shard_map(
        shards, mesh=mesh, in_specs=placed, out_specs=P("row", "col"), check_vma=False
    )
```

time: 803 us -> 133 us (0.17)
  waiting for transfers between devices: 723 us -> 0 us
  Pallas kernels: 0 us -> 122 us
  matrix products: 50.4 us -> 7.64 us
  between operations: 13.6 us -> 0.01 us
    reduce_scatter x4 -> x0, waiting for transfers between devices: 304 us -> none  [the longest x2 185 us: shards(): lax.psum_scatter(lax.dot_general(rounded, factor_rows, (((0,), (0,)), (()...]
    all_gather x5 -> x0, waiting for transfers between devices: 269 us -> none  [the longest x2 136 us: shards(): lax.all_gather(summed_cols, 'row', axis=0, tiled=True)]
    psum x1 -> x0, waiting for transfers between devices: 149 us -> none  [spread(): return lax.psum(block, axis)]
    pallas_call x0 -> x1, Pallas kernels: none -> 122 us  [shards(): pl.pallas_call(cycle, out_shape=(jax.ShapeDtypeStruct((row_tile, AUX), BF...]
    dot_general x6 -> x1, matrix products: 50.4 us -> 7.64 us  [shards(): residual = lax.dot_general(dr, dc, NT, preferred_element_type=F32)]
  transfers between devices with their start and end apart: 10 -> 0, of which waited for: 10 -> 0; matrix products, arithmetic and copies ran while one was open for 3% -> 0% of each run, Pallas kernels for 0% -> 0%
where the time goes in v2:
time: 133 us; the launch traced here: 132 us
  Pallas kernels  122 us (92%)
  matrix products  7.64 us (6%)
  local copies, waits for them, and re-layouts  3.15 us (2%)
    pallas_call x1, Pallas kernels, shards(): pl.pallas_call(cycle, out_shape=(jax.ShapeDtypeStruct((row_tile, AUX), BF...  122 us
    dot_general x1, matrix products, shards(): residual = lax.dot_general(dr, dc, NT, preferred_element_type=F32)  7.64 us

profile of v2, /device:TPU:1, one launch (start us, length us, event | category | flops | bytes accessed | tf_op | source)
XLA Modules:
  0.0 132.4 jit_solution(16324946207389531105)
XLA Ops:
  0.0 0.7 dynamic_slice.6
  0.7 0.7 dynamic_slice.7
  1.4 0.0 copy-start
  1.4 0.9 copy-done
  2.3 0.0 copy-start.1
  2.3 0.8 copy-done.1
  3.2 121.6 %cycle.1 = (bf16[1024,768]{1,0:T(8,128)(2,1)S(1)}, bf16[2048,768]{1,0:T(8,128)(2,1)}) custom-call(f32[1024,2048]{1,0:T(8,128)} %amp.1, bf16[128,768]{1,0:T(8,128)(2,1)S(1)} %copy-done, f32[128,128]{1,0:T(8,128)S(1)} %bitcast.3), custom_call_target="tpu_custom_call" | custom-call | tf_op jit(solution)/shard_map/cycle/pallas_call | solution.py:515
  124.7 7.6 %add_divide_fusion = f32[1024,2048]{1,0:T(8,128)} fusion(bf16[1024,768]{1,0:T(8,128)(2,1)S(1)} %get-tuple-element.7, bf16[2048,768]{1,0:T(8,128)(2,1)} %get-tuple-element.8, f32[2048]{0:T(1024)S(1)} %dynamic_slice.7, f32[1024]{0:T(1024)S(1)} %dynamic_slice.6), kind=kOutput, calls=%fused_computation | convolution fusion | flops 3227516928 | bytes 13119488 | tf_op jit(solution)/shard_map/dot_general | solution.py:552
Async XLA Ops:
  1.4 0.9 copy-start
  2.3 0.8 copy-start.1

commit v3 on v2

--- a/solution.py
+++ b/solution.py
@@ -180,6 +180,38 @@
         total = self.collect(1)
         self.got(6, self.inz, self.line.z)
         return total + self.inz[...].astype(F32)
+
+
+def spread_energies(energy, e_row, e_col):
+    row, col = lax.axis_index("row"), lax.axis_index("col")
+    for j in range(8):
+        v = energy[pl.ds(row * 8 + j, 1), :]
+        e_row[j * 128 : (j + 1) * 128, :] = jnp.broadcast_to(v, (128, 128)).T
+    for j in range(16):
+        e_col[:, j * 128 : (j + 1) * 128] = energy[pl.ds(col * 16 + j, 1), :]
+
+
+def tile(dr, dc, e_row, e_col, rows, cols):
+    residual = lax.dot_general(dr[rows, :], dc[cols, :], NT, preferred_element_type=F32)
+    den = jnp.concatenate([e_row[rows, :]] * (residual.shape[1] // 128), axis=1) + e_col[:, cols]
+    return -COUPLING * residual / den
+
+
+def finish(dr, dc, energy, out, stage, e_row, e_col, sem):
+    spread_energies(energy, e_row, e_col)
+
+    def put(i):
+        return pltpu.make_async_copy(stage.at[i % 2], out.at[pl.ds(i * 128, 128), :], sem.at[i % 2])
+
+    for i in range(8):
+        if i >= 2:
+            put(i - 2).wait()
+        for j in range(4):
+            cols = slice(j * 512, (j + 1) * 512)
+            stage[i % 2, :, cols] = tile(dr, dc, e_row, e_col, slice(i * 128, (i + 1) * 128), cols)
+        put(i).start()
+    put(6).wait()
+    put(7).wait()
 
 
 def cycle(
@@ -257,11 +289,7 @@
         greet(turn_to)
         greet(turn_from)
 
-    for j in range(8):
-        v = energy[pl.ds(row * 8 + j, 1), :]
-        e_row[j * 128 : (j + 1) * 128, :] = jnp.broadcast_to(v, (128, 128)).T
-    for j in range(16):
-        e_col[:, j * 128 : (j + 1) * 128] = energy[pl.ds(col * 16 + j, 1), :]
+    spread_energies(energy, e_row, e_col)
 
     @pl.when(moves)
     def _():
@@ -393,9 +421,18 @@
         rsy.pair()
         rsx.pair()
 
-        hx = [Gather(line_x, dr, k, agx_s.at[1 + 2 * it + k], agx_r.at[1 + 2 * it + k]) for k in range(2)]
+        hx = [
+            Gather(
+                line_x, dr, k, agx_s.at[1 + 2 * it + k], agx_r.at[1 + 2 * it + k],
+                relay_own=True, relay_pair=k == 0,
+            )
+            for k in range(2)
+        ]
         hy = [
-            Gather(line_y, dc, k, agy_s.at[1 + 2 * it + k], agy_r.at[1 + 2 * it + k], half_c, other_c)
+            Gather(
+                line_y, dc, k, agy_s.at[1 + 2 * it + k], agy_r.at[1 + 2 * it + k], half_c, other_c,
+                relay_own=True, relay_pair=k == 1,
+            )
             for k in range(2)
         ]
         r0, r1 = part_of(dr, mine_r, 0), part_of(dr, mine_r, 1)
@@ -445,20 +482,20 @@
         hy[0].start()
         hy[1].near()
         hx[0].near()
+        hy[1].near_pair()
+        hx[0].near_pair()
+        hy[0].pair()
+        hx[1].pair()
         hy[1].far()
         hx[0].far()
-        hy[1].near_pair()
-        hx[0].near_pair()
-        hx[1].pair()
-        hy[0].pair()
+        hy[0].near()
+        hx[1].near()
         hy[1].far_pair()
         hx[0].far_pair()
-        hy[0].near()
-        hx[1].near()
+        hy[0].near_pair()
+        hx[1].near_pair()
         hy[0].far()
         hx[1].far()
-        hy[0].near_pair()
-        hx[1].near_pair()
         hy[0].far_pair()
         hx[1].far_pair()
         hy[1].from_core()
@@ -471,11 +508,7 @@
                 at_rows = pl.ds(pl.multiple_of(i * 256, 256), 256)
                 for j in range(4):
                     cols = slice(j * 512, (j + 1) * 512)
-                    residual = lax.dot_general(
-                        dr0[at_rows, :], dc0[cols, :], NT, preferred_element_type=F32
-                    )
-                    den = jnp.concatenate([e_row[at_rows, :]] * 4, axis=1) + e_col[:, cols]
-                    a[at_rows, cols] = (-COUPLING * residual / den).astype(BF16)
+                    a[at_rows, cols] = tile(dr0, dc0, e_row, e_col, at_rows, cols).astype(BF16)
 
         for i in range(4):
             core_copy(i).wait_send()
@@ -512,6 +545,7 @@
             pltpu.VMEM((2, SLOT, K), BF16),
         ]
 
+    energy = energies.reshape(128, 128)
     dr, dc = pl.pallas_call(
         cycle,
         out_shape=(
@@ -542,15 +576,25 @@
             dma(2, 4), dma(2, 4),
         ],
         compiler_params=pltpu.CompilerParams(
-            collective_id=0, has_side_effects=True, vmem_limit_bytes=50 * 1024 * 1024
+            collective_id=0, has_side_effects=True, vmem_limit_bytes=46 * 1024 * 1024
         ),
         name="cycle",
-    )(amplitudes, factors, energies.reshape(128, 128))
-
-    row_energy = lax.dynamic_slice_in_dim(energies, lax.axis_index("row") * row_tile, row_tile)
-    col_energy = lax.dynamic_slice_in_dim(energies, lax.axis_index("col") * col_tile, col_tile)
-    residual = lax.dot_general(dr, dc, NT, preferred_element_type=F32)
-    return -COUPLING * residual / (row_energy[:, None] + col_energy[None, :])
+    )(amplitudes, factors, energy)
+
+    return pl.pallas_call(
+        finish,
+        out_shape=jax.ShapeDtypeStruct((row_tile, col_tile), F32),
+        in_specs=[vmem, vmem, vmem],
+        out_specs=pl.BlockSpec(memory_space=pl.ANY),
+        scratch_shapes=[
+            pltpu.VMEM((2, 128, col_tile), F32),
+            pltpu.VMEM((row_tile, 128), F32),
+            pltpu.VMEM((1, col_tile), F32),
+            dma(2),
+        ],
+        compiler_params=pltpu.CompilerParams(vmem_limit_bytes=20 * 1024 * 1024),
+        name="finish",
+    )(dr, dc, energy)
 
 
 def solution(mesh):

time: 133 us -> 126 us (0.947)
  matrix products: 7.64 us -> 0 us
  Pallas kernels: 122 us -> 124 us
  local copies, waits for them, and re-layouts: 3.15 us -> 1.77 us
    pallas_call x0 -> x1, Pallas kernels: none -> 10.1 us  [shards(): pl.pallas_call(finish, out_shape=jax.ShapeDtypeStruct((row_tile, col_tile...]
    dot_general x1 -> x0, matrix products: 7.64 us -> none  [shards(): residual = lax.dot_general(dr, dc, NT, preferred_element_type=F32)]
    pallas_call x1, Pallas kernels: 122 us -> 114 us  [shards(): pl.pallas_call(cycle, out_shape=(jax.ShapeDtypeStruct((row_tile, AUX), BF...]
    dynamic_slice x2 -> x0, local copies, waits for them, and re-layouts: 1.38 us -> none  [the longest x1 0.7 us: shards(): lax.dynamic_slice_in_dim(energies, lax.axis_index('col') * col_tile, col_...]
where the time goes in v3:
time: 126 us
  Pallas kernels  124 us (98%)
  local copies, waits for them, and re-layouts  1.77 us (1%)
    pallas_call x1, Pallas kernels, shards(): pl.pallas_call(cycle, out_shape=(jax.ShapeDtypeStruct((row_tile, AUX), BF...  114 us
    pallas_call x1, Pallas kernels, shards(): pl.pallas_call(finish, out_shape=jax.ShapeDtypeStruct((row_tile, col_tile...  10.1 us

profile of v3, /device:TPU:1, one launch (start us, length us, event | category | flops | bytes accessed | tf_op | source)
XLA Modules:
  0.0 126.0 jit_solution(16684982327599684218)
XLA Ops:
  0.0 0.0 copy-start
  0.0 0.8 copy-done
  0.8 0.0 copy-start.1
  0.8 0.9 copy-done.1
  1.8 114.0 %cycle.1 = (bf16[1024,768]{1,0:T(8,128)(2,1)S(1)}, bf16[2048,768]{1,0:T(8,128)(2,1)S(1)}) custom-call(f32[1024,2048]{1,0:T(8,128)} %amp.1, bf16[128,768]{1,0:T(8,128)(2,1)S(1)} %copy-done.1, f32[128,128]{1,0:T(8,128)S(1)} %bitcast.1), custom_call_target="tpu_custom_call" | custom-call | tf_op jit(solution)/shard_map/cycle/pallas_call | solution.py:549
  115.8 10.1 %finish.1 = f32[1024,2048]{1,0:T(8,128)} custom-call(bf16[1024,768]{1,0:T(8,128)(2,1)S(1)} %get-tuple-element.7.dr, bf16[2048,768]{1,0:T(8,128)(2,1)S(1)} %get-tuple-element.8.dc, f32[128,128]{1,0:T(8,128)S(1)} %bitcast.2), custom_call_target="tpu_custom_call" | custom-call | tf_op jit(solution)/shard_map/finish/pallas_call | solution.py:584
Async XLA Ops:
  0.0 0.8 copy-start
  0.8 0.9 copy-start.1

commit v4 on v3

--- a/solution.py
+++ b/solution.py
@@ -141,11 +141,11 @@
             self.arrived(7, ln.so_z, ln.o)
         self.to_core(7, ln.so_z)
 
-    def from_core(self):
+    def from_core(self, first=0, last=8):
         ln = self.line
         order = (ln.own, ln.own_z, ln.sm, ln.sp, ln.sm_z, ln.sp_z, ln.so, ln.so_z)
-        for i, slot in enumerate(order):
-            self.got(9 + i, part_of(self.buf, self.other + slot, self.k), ln.core)
+        for i in range(first, last):
+            self.got(9 + i, part_of(self.buf, self.other + order[i], self.k), ln.core)
 
 
 class Reduce(Exchange):
@@ -191,35 +191,33 @@
         e_col[:, j * 128 : (j + 1) * 128] = energy[pl.ds(col * 16 + j, 1), :]
 
 
-def tile(dr, dc, e_row, e_col, rows, cols):
-    residual = lax.dot_general(dr[rows, :], dc[cols, :], NT, preferred_element_type=F32)
-    den = jnp.concatenate([e_row[rows, :]] * (residual.shape[1] // 128), axis=1) + e_col[:, cols]
+def tile(dr, dc, e_row, e_col):
+    residual = lax.dot_general(dr, dc, NT, preferred_element_type=F32)
+    den = jnp.concatenate([e_row] * (residual.shape[1] // 128), axis=1) + e_col
     return -COUPLING * residual / den
 
 
-def finish(dr, dc, energy, out, stage, e_row, e_col, sem):
-    spread_energies(energy, e_row, e_col)
-
+def finish(dr, dc, e_row, e_col, out, stage, sem):
     def put(i):
-        return pltpu.make_async_copy(stage.at[i % 2], out.at[pl.ds(i * 128, 128), :], sem.at[i % 2])
-
-    for i in range(8):
+        return pltpu.make_async_copy(stage.at[i % 2], out.at[pl.ds(i * 256, 256), :], sem.at[i % 2])
+
+    for i in range(4):
         if i >= 2:
             put(i - 2).wait()
         for j in range(4):
             cols = slice(j * 512, (j + 1) * 512)
-            stage[i % 2, :, cols] = tile(dr, dc, e_row, e_col, slice(i * 128, (i + 1) * 128), cols)
+            rows = slice(i * 256, (i + 1) * 256)
+            stage[i % 2, :, cols] = tile(dr[rows, :], dc[cols, :], e_row[rows, :], e_col[:, cols])
         put(i).start()
-    put(6).wait()
-    put(7).wait()
+    put(2).wait()
+    put(3).wait()
 
 
 def cycle(
-    amp, own, energy, dr1, dc1,
-    a, stage, fr, fc, own_c, dr0, dc0, part_r, part_c, core_out, core_in,
+    amp, own_hbm, energy_hbm, dr1, dc1, e_row, e_col,
+    a, stage, own, energy, fr, fc, own_c, dr0, dc0, part_r, part_c, core_out, core_in,
     x_out, x_outz, x_in, x_inz, y_out, y_outz, y_in, y_inz,
-    e_row, e_col,
-    amp_sem, turn_s, turn_r, agx_s, agx_r, agy_s, agy_r, rsx_s, rsx_r, rsy_s, rsy_r, co_s, co_r,
+    amp_sem, in_sem, turn_s, turn_r, agx_s, agx_r, agy_s, agy_r, rsx_s, rsx_r, rsy_s, rsy_r, co_s, co_r,
 ):
     row, col = lax.axis_index("row"), lax.axis_index("col")
     core, chip_row = lax.rem(row, 2), row // 2
@@ -271,6 +269,10 @@
     def amp_copy(i):
         return pltpu.make_async_copy(amp.at[pl.ds(i * 256, 256), :], stage.at[i % 2], amp_sem.at[i % 2])
 
+    own_copy = pltpu.make_async_copy(own_hbm, own, in_sem.at[0])
+    energy_copy = pltpu.make_async_copy(energy_hbm, energy, in_sem.at[1])
+    own_copy.start()
+    energy_copy.start()
     amp_copy(0).start()
     amp_copy(1).start()
 
@@ -289,7 +291,7 @@
         greet(turn_to)
         greet(turn_from)
 
-    spread_energies(energy, e_row, e_col)
+    own_copy.wait()
 
     @pl.when(moves)
     def _():
@@ -299,8 +301,8 @@
     def _():
         pl.semaphore_wait(barrier, 9)
 
-    gx = Gather(line_x, fr, None, agx_s.at[0], agx_r.at[0])
-    gy = Gather(line_y, fc, None, agy_s.at[0], agy_r.at[0], half_c, other_c)
+    gx = Gather(line_x, fr, None, agx_s.at[0], agx_r.at[0], relay_own=True)
+    gy = Gather(line_y, fc, None, agy_s.at[0], agy_r.at[0], half_c, other_c, relay_own=True)
     own0, own1 = own.at[:, pl.ds(0, K)], own.at[:, pl.ds(K, K)]
     turn_f0 = turn(0, own0, part_of(fc, half_c + col), turn_to)
     turn_f1 = turn(1, own1, own_c, turn_to)
@@ -322,6 +324,8 @@
         part_of(fc, mine_c)[...] = own0[...]
         own_c[...] = own1[...]
 
+    energy_copy.wait()
+    spread_energies(energy, e_row, e_col)
     for i in range(4):
         amp_copy(i).wait()
         a[i * 256 : (i + 1) * 256, :] = stage[i % 2].astype(BF16)
@@ -336,9 +340,10 @@
 
     gy.start()
     gx.near()
-    gx.far()
     gy.pair()
     gx.near_pair()
+    gx.far()
+    gy.near()
     gx.far_pair()
 
     def mm_rows(s):
@@ -349,6 +354,24 @@
         lhs = [a[:, pl.ds(pl.multiple_of((half + i) * SLOT, SLOT), SLOT)] for i in (s, s_z)]
         lhs = jnp.concatenate(lhs, axis=1)
         return lax.dot_general(lhs, fr[...], TN, preferred_element_type=F32) * INV_ROOT
+
+    def new_tile(i, j):
+        rows = pl.ds(pl.multiple_of(lax.rem(x + i, 4) * 256, 256), 256)
+        first = lax.rem(x + y + j + 4 - first_y, 4) * 256
+        cols = [pl.ds(pl.multiple_of(h * 1024 + first, 256), 256) for h in range(2)]
+        value = tile(
+            dr0[rows, :],
+            jnp.concatenate([dc0[c, :] for c in cols], axis=0),
+            e_row[rows, :],
+            jnp.concatenate([e_col[:, c] for c in cols], axis=1),
+        ).astype(BF16)
+        for h in range(2):
+            a[rows, cols[h]] = value[:, h * 256 : (h + 1) * 256]
+
+    def new_tiles(t):
+        @pl.loop(0, 3)
+        def _(n):
+            new_tile(t + t // 2, n + n // 2)
 
     pairs_y = (
         (line_y.so, line_y.so_z), (line_y.sp, line_y.sp_z), (line_y.sm, line_y.sm_z), (line_y.own, line_y.own_z),
@@ -380,15 +403,14 @@
         if it == 0:
             other_half(0)
             other_half(1)
-            gy.near()
-            gy.far()
+            gy.near_pair()
             other_half(2)
             other_half(3)
             own_half(0)
             rsy.give(2)
             own_half(1)
             rsy.give(0)
-            gy.near_pair()
+            gy.far()
             gy.far_pair()
             own_half(2)
             rsy.give(1)
@@ -494,21 +516,32 @@
         hx[0].far_pair()
         hy[0].near_pair()
         hx[1].near_pair()
-        hy[0].far()
-        hx[1].far()
-        hy[0].far_pair()
-        hx[1].far_pair()
-        hy[1].from_core()
-        hy[0].from_core()
-
         if it == 0:
+            hy[1].from_core()
+            hy[0].from_core(0, 6)
+            new_tiles(0)
+            hy[0].far()
+            hx[1].far()
+            new_tiles(1)
+            hy[0].far_pair()
+            hx[1].far_pair()
+            new_tiles(2)
+            hy[0].from_core(6, 8)
 
             @pl.loop(0, 4)
-            def _(i):
-                at_rows = pl.ds(pl.multiple_of(i * 256, 256), 256)
-                for j in range(4):
-                    cols = slice(j * 512, (j + 1) * 512)
-                    a[at_rows, cols] = tile(dr0, dc0, e_row, e_col, at_rows, cols).astype(BF16)
+            def _(n):
+                new_tile(2, n)
+
+            @pl.loop(0, 3)
+            def _(n):
+                new_tile(n + n // 2, 2)
+        else:
+            hy[0].far()
+            hx[1].far()
+            hy[0].far_pair()
+            hx[1].far_pair()
+            hy[1].from_core()
+            hy[0].from_core()
 
         for i in range(4):
             core_copy(i).wait_send()
@@ -546,17 +579,22 @@
         ]
 
     energy = energies.reshape(128, 128)
-    dr, dc = pl.pallas_call(
+    hbm = pl.BlockSpec(memory_space=pltpu.MemorySpace.HBM)
+    dr, dc, e_row, e_col = pl.pallas_call(
         cycle,
         out_shape=(
             jax.ShapeDtypeStruct((row_tile, AUX), BF16),
             jax.ShapeDtypeStruct((col_tile, AUX), BF16),
+            jax.ShapeDtypeStruct((row_tile, 128), F32),
+            jax.ShapeDtypeStruct((1, col_tile), F32),
         ),
-        in_specs=[pl.BlockSpec(memory_space=pl.ANY), vmem, vmem],
-        out_specs=(vmem, vmem),
+        in_specs=[hbm, hbm, hbm],
+        out_specs=(vmem, vmem, vmem, vmem),
         scratch_shapes=[
             pltpu.VMEM((row_tile, col_tile), BF16),
             pltpu.VMEM((2, 256, col_tile), F32),
+            pltpu.VMEM((SLOT, AUX), BF16),
+            pltpu.VMEM((128, 128), F32),
             pltpu.VMEM((row_tile, K), BF16),
             pltpu.VMEM((col_tile, K), BF16),
             pltpu.VMEM((SLOT, K), BF16),
@@ -568,9 +606,7 @@
             pltpu.VMEM((2, 4, 256, K), BF16),
             *line_buffers(),
             *line_buffers(),
-            pltpu.VMEM((row_tile, 128), F32),
-            pltpu.VMEM((1, col_tile), F32),
-            dma(2), dma(6), dma(6),
+            dma(2), dma(2), dma(6), dma(6),
             dma(5, 9), dma(5, 9), dma(5, 17), dma(5, 17),
             dma(2, 7), dma(2, 7), dma(2, 7), dma(2, 7),
             dma(2, 4), dma(2, 4),
@@ -579,22 +615,17 @@
             collective_id=0, has_side_effects=True, vmem_limit_bytes=46 * 1024 * 1024
         ),
         name="cycle",
-    )(amplitudes, factors, energy)
+    )(*(pltpu.with_memory_space_constraint(v, pltpu.MemorySpace.HBM) for v in (amplitudes, factors, energy)))
 
     return pl.pallas_call(
         finish,
         out_shape=jax.ShapeDtypeStruct((row_tile, col_tile), F32),
-        in_specs=[vmem, vmem, vmem],
+        in_specs=[vmem, vmem, vmem, vmem],
         out_specs=pl.BlockSpec(memory_space=pl.ANY),
-        scratch_shapes=[
-            pltpu.VMEM((2, 128, col_tile), F32),
-            pltpu.VMEM((row_tile, 128), F32),
-            pltpu.VMEM((1, col_tile), F32),
-            dma(2),
-        ],
+        scratch_shapes=[pltpu.VMEM((2, 256, col_tile), F32), dma(2)],
         compiler_params=pltpu.CompilerParams(vmem_limit_bytes=20 * 1024 * 1024),
         name="finish",
-    )(dr, dc, energy)
+    )(dr, dc, e_row, e_col)
 
 
 def solution(mesh):

time: 126 us -> 121 us (0.960)
  Pallas kernels: 124 us -> 121 us
  local copies, waits for them, and re-layouts: 1.77 us -> 0 us
    pallas_call x1, Pallas kernels: 10.1 us -> 5.71 us  [shards(): pl.pallas_call(finish, out_shape=jax.ShapeDtypeStruct((row_tile, col_tile...]
    unnamed x4 -> x0, local copies, waits for them, and re-layouts: 1.77 us -> none
where the time goes in v4:
time: 121 us
  Pallas kernels  121 us (100%)
    pallas_call x1, Pallas kernels, shards(): pl.pallas_call(cycle, out_shape=(jax.ShapeDtypeStruct((row_tile, AUX), BF...  115 us
    pallas_call x1, Pallas kernels, shards(): pl.pallas_call(finish, out_shape=jax.ShapeDtypeStruct((row_tile, col_tile...  5.71 us

profile of v4, /device:TPU:1, one launch (start us, length us, event | category | flops | bytes accessed | tf_op | source)
XLA Modules:
  0.0 120.8 jit_solution(4634745180543430507)
XLA Ops:
  0.0 114.9 %cycle.1 = (bf16[1024,768]{1,0:T(8,128)(2,1)S(1)}, bf16[2048,768]{1,0:T(8,128)(2,1)S(1)}, f32[1024,128]{1,0:T(8,128)S(1)}, f32[1,2048]{1,0:T(1,128)S(1)}) custom-call(f32[1024,2048]{1,0:T(8,128)} %amp.1, bf16[128,768]{1,0:T(8,128)(2,1)} %own_hbm.1, f32[128,128]{1,0:T(8,128)} %bitcast.1), custom_call_target="tpu_custom_call" | custom-call | tf_op jit(solution)/shard_map/cycle/pallas_call | solution.py:583
  114.9 5.7 %finish.1 = f32[1024,2048]{1,0:T(8,128)} custom-call(bf16[1024,768]{1,0:T(8,128)(2,1)S(1)} %get-tuple-element.9.dr, bf16[2048,768]{1,0:T(8,128)(2,1)S(1)} %get-tuple-element.10.dc, f32[1024,128]{1,0:T(8,128)S(1)} %get-tuple-element.11.e_row, f32[1,2048]{1,0:T(1,128)S(1)} %get-tuple-element.12.e_col), custom_call_target="tpu_custom_call" | custom-call | tf_op jit(solution)/shard_map/finish/pallas_call | solution.py:620

commit v5 on v4

--- a/solution.py
+++ b/solution.py
@@ -215,7 +215,7 @@
 
 def cycle(
     amp, own_hbm, energy_hbm, dr1, dc1, e_row, e_col,
-    a, stage, own, energy, fr, fc, own_c, dr0, dc0, part_r, part_c, core_out, core_in,
+    a, stage, own, energy, fr, fc, own_c, dr0, dc0, part_r, part_c, core_out, core_in, weight,
     x_out, x_outz, x_in, x_inz, y_out, y_outz, y_in, y_inz,
     amp_sem, in_sem, turn_s, turn_r, agx_s, agx_r, agy_s, agy_r, rsx_s, rsx_r, rsy_s, rsy_r, co_s, co_r,
 ):
@@ -301,7 +301,7 @@
     def _():
         pl.semaphore_wait(barrier, 9)
 
-    gx = Gather(line_x, fr, None, agx_s.at[0], agx_r.at[0], relay_own=True)
+    gx = Gather(line_x, fr, None, agx_s.at[0], agx_r.at[0], relay_own=True, relay_pair=True)
     gy = Gather(line_y, fc, None, agy_s.at[0], agy_r.at[0], half_c, other_c, relay_own=True)
     own0, own1 = own.at[:, pl.ds(0, K)], own.at[:, pl.ds(K, K)]
     turn_f0 = turn(0, own0, part_of(fc, half_c + col), turn_to)
@@ -359,19 +359,15 @@
         rows = pl.ds(pl.multiple_of(lax.rem(x + i, 4) * 256, 256), 256)
         first = lax.rem(x + y + j + 4 - first_y, 4) * 256
         cols = [pl.ds(pl.multiple_of(h * 1024 + first, 256), 256) for h in range(2)]
-        value = tile(
-            dr0[rows, :],
-            jnp.concatenate([dc0[c, :] for c in cols], axis=0),
-            e_row[rows, :],
-            jnp.concatenate([e_col[:, c] for c in cols], axis=1),
-        ).astype(BF16)
+        residual = lax.dot_general(
+            dr0[rows, :], jnp.concatenate([dc0[c, :] for c in cols], axis=0), NT, preferred_element_type=F32
+        )
         for h in range(2):
-            a[rows, cols[h]] = value[:, h * 256 : (h + 1) * 256]
-
-    def new_tiles(t):
-        @pl.loop(0, 3)
-        def _(n):
-            new_tile(t + t // 2, n + n // 2)
+            a[rows, cols[h]] = (residual[:, h * 256 : (h + 1) * 256] * weight[rows, cols[h]]).astype(BF16)
+
+    def new_tiles(i):
+        for j in (0, 1, 3):
+            new_tile(i, j)
 
     pairs_y = (
         (line_y.so, line_y.so_z), (line_y.sp, line_y.sp_z), (line_y.sm, line_y.sm_z), (line_y.own, line_y.own_z),
@@ -426,21 +422,30 @@
         else:
             mm_rows(line_x.so)
             rsx.give(2)
+            for i in (0, 1, 3):
+                new_tile(i, 2)
             for i in range(4):
                 other_half(i)
             own_half(0)
             rsy.give(2)
+            mm_rows(line_x.sp)
+            rsx.give(0)
             own_half(1)
             rsy.give(0)
+            mm_rows(line_x.sm)
+            rsx.give(1)
             own_half(2)
             rsy.give(1)
-            mm_rows(line_x.sp)
-            rsx.give(0)
-            mm_rows(line_x.sm)
-            rsx.give(1)
             own_half(3)
             mm_rows(line_x.own)
         rsy.pair()
+        if it == 0:
+
+            @pl.loop(0, 8)
+            def _(i):
+                rows = pl.ds(pl.multiple_of(i * 128, 128), 128)
+                weight[rows, :] = -COUPLING / (jnp.concatenate([e_row[rows, :]] * 16, axis=1) + e_col[...])
+
         rsx.pair()
 
         hx = [
@@ -525,16 +530,10 @@
             new_tiles(1)
             hy[0].far_pair()
             hx[1].far_pair()
-            new_tiles(2)
+            new_tiles(3)
             hy[0].from_core(6, 8)
-
-            @pl.loop(0, 4)
-            def _(n):
-                new_tile(2, n)
-
-            @pl.loop(0, 3)
-            def _(n):
-                new_tile(n + n // 2, 2)
+            for j in (0, 1, 3, 2):
+                new_tile(2, j)
         else:
             hy[0].far()
             hx[1].far()
@@ -604,6 +603,7 @@
             pltpu.VMEM((row_tile, K), F32),
             pltpu.VMEM((4, 256, K), BF16),
             pltpu.VMEM((2, 4, 256, K), BF16),
+            pltpu.VMEM((row_tile, col_tile), F32),
             *line_buffers(),
             *line_buffers(),
             dma(2), dma(2), dma(6), dma(6),

time: 121 us -> 117 us (0.967)
  Pallas kernels: 121 us -> 117 us
    pallas_call x1, Pallas kernels: 115 us -> 111 us  [shards(): pl.pallas_call(cycle, out_shape=(jax.ShapeDtypeStruct((row_tile, AUX), BF...]
where the time goes in v5:
time: 117 us
  Pallas kernels  117 us (100%)
    pallas_call x1, Pallas kernels, shards(): pl.pallas_call(cycle, out_shape=(jax.ShapeDtypeStruct((row_tile, AUX), BF...  111 us
    pallas_call x1, Pallas kernels, shards(): pl.pallas_call(finish, out_shape=jax.ShapeDtypeStruct((row_tile, col_tile...  5.72 us

profile of v5, /device:TPU:1, one launch (start us, length us, event | category | flops | bytes accessed | tf_op | source)
XLA Modules:
  0.0 116.9 jit_solution(4637204317396264058)
XLA Ops:
  0.0 111.0 %cycle.1 = (bf16[1024,768]{1,0:T(8,128)(2,1)S(1)}, bf16[2048,768]{1,0:T(8,128)(2,1)S(1)}, f32[1024,128]{1,0:T(8,128)S(1)}, f32[1,2048]{1,0:T(1,128)S(1)}) custom-call(f32[1024,2048]{1,0:T(8,128)} %amp.1, bf16[128,768]{1,0:T(8,128)(2,1)} %own_hbm.1, f32[128,128]{1,0:T(8,128)} %bitcast.1), custom_call_target="tpu_custom_call" | custom-call | tf_op jit(solution)/shard_map/cycle/pallas_call | solution.py:582
  111.0 5.7 %finish.1 = f32[1024,2048]{1,0:T(8,128)} custom-call(bf16[1024,768]{1,0:T(8,128)(2,1)S(1)} %get-tuple-element.9.dr, bf16[2048,768]{1,0:T(8,128)(2,1)S(1)} %get-tuple-element.10.dc, f32[1024,128]{1,0:T(8,128)S(1)} %get-tuple-element.11.e_row, f32[1,2048]{1,0:T(1,128)S(1)} %get-tuple-element.12.e_col), custom_call_target="tpu_custom_call" | custom-call | tf_op jit(solution)/shard_map/finish/pallas_call | solution.py:620

commit v6 on v5

--- a/solution.py
+++ b/solution.py
@@ -85,7 +85,9 @@
 
     def start(self, src=None):
         ln = self.line
-        self.push(2, ln.own, ln.z, src=src)
+        for h in range(2):
+            half = None if src is None else src.at[pl.ds(h * HALF, HALF), :]
+            self.push(17 * h + 2 * (1 - h), ln.own, ln.z, h * HALF, HALF, src=half)
         if not self.relay_own:
             self.push(5, ln.own, ln.o, src=src)
         self.push(0, ln.own, ln.p, src=src)
@@ -94,11 +96,12 @@
 
     def pair(self):
         ln = self.line
-        self.arrived(2, ln.own_z, ln.z)
-        if not self.relay_pair:
-            self.push(7, ln.own_z, ln.o)
-        self.push(3, ln.own_z, ln.p)
-        self.push(4, ln.own_z, ln.m)
+        for h, (i, to_p, to_m) in enumerate(((2, 3, 4), (17, 18, 19))):
+            self.arrived(i, ln.own_z, ln.z, h * HALF, HALF)
+            if not self.relay_pair:
+                self.push(7 + h, ln.own_z, ln.o, h * HALF, HALF)
+            self.push(to_p, ln.own_z, ln.p, h * HALF, HALF)
+            self.push(to_m, ln.own_z, ln.m, h * HALF, HALF)
         self.to_core(1, ln.own_z)
 
     def near(self):
@@ -114,13 +117,15 @@
 
     def near_pair(self):
         ln = self.line
-        self.arrived(3, ln.sm_z, ln.m)
+        self.arrived(3, ln.sm_z, ln.m, 0, HALF)
         if self.relay_pair:
             self.push(7, ln.sm_z, ln.p, 0, HALF)
-        self.to_core(4, ln.sm_z)
-        self.arrived(4, ln.sp_z, ln.p)
+        self.arrived(19, ln.sp_z, ln.p, HALF, HALF)
         if self.relay_pair:
             self.push(8, ln.sp_z, ln.m, HALF, HALF)
+        self.arrived(18, ln.sm_z, ln.m, HALF, HALF)
+        self.to_core(4, ln.sm_z)
+        self.arrived(4, ln.sp_z, ln.p, 0, HALF)
         self.to_core(5, ln.sp_z)
 
     def far(self):
@@ -138,7 +143,8 @@
             self.arrived(7, ln.so_z, ln.m, 0, HALF)
             self.arrived(8, ln.so_z, ln.p, HALF, HALF)
         else:
-            self.arrived(7, ln.so_z, ln.o)
+            self.arrived(7, ln.so_z, ln.o, 0, HALF)
+            self.arrived(8, ln.so_z, ln.o, HALF, HALF)
         self.to_core(7, ln.so_z)
 
     def from_core(self, first=0, last=8):
@@ -291,7 +297,14 @@
         greet(turn_to)
         greet(turn_from)
 
+    def take_amp(i):
+        amp_copy(i).wait()
+        a[i * 256 : (i + 1) * 256, :] = stage[i % 2].astype(BF16)
+        if i + 2 < 4:
+            amp_copy(i + 2).start()
+
     own_copy.wait()
+    take_amp(0)
 
     @pl.when(moves)
     def _():
@@ -312,11 +325,6 @@
         turn_f0.start()
 
     gx.start(src=own1)
-
-    @pl.when(moves)
-    def _():
-        turn_f1.start()
-
     part_of(fr, mine_r)[...] = own1[...]
 
     @pl.when(stays)
@@ -324,15 +332,12 @@
         part_of(fc, mine_c)[...] = own0[...]
         own_c[...] = own1[...]
 
+    take_amp(1)
+    take_amp(2)
+    gx.pair()
+    take_amp(3)
     energy_copy.wait()
     spread_energies(energy, e_row, e_col)
-    for i in range(4):
-        amp_copy(i).wait()
-        a[i * 256 : (i + 1) * 256, :] = stage[i % 2].astype(BF16)
-        if i + 2 < 4:
-            amp_copy(i + 2).start()
-
-    gx.pair()
 
     @pl.when(moves)
     def _():
@@ -345,6 +350,11 @@
     gx.far()
     gy.near()
     gx.far_pair()
+
+    @pl.when(moves)
+    def _():
+        turn_f1.start()
+
 
     def mm_rows(s):
         at_rows = pl.ds(pl.multiple_of((s // 2) * 256, 256), 256)
@@ -424,18 +434,20 @@
             rsx.give(2)
             for i in (0, 1, 3):
                 new_tile(i, 2)
-            for i in range(4):
-                other_half(i)
+            other_half(0)
+            other_half(1)
             own_half(0)
             rsy.give(2)
+            other_half(2)
+            own_half(1)
+            rsy.give(0)
             mm_rows(line_x.sp)
             rsx.give(0)
-            own_half(1)
-            rsy.give(0)
+            other_half(3)
+            own_half(2)
+            rsy.give(1)
             mm_rows(line_x.sm)
             rsx.give(1)
-            own_half(2)
-            rsy.give(1)
             own_half(3)
             mm_rows(line_x.own)
         rsy.pair()
@@ -607,7 +619,7 @@
             *line_buffers(),
             *line_buffers(),
             dma(2), dma(2), dma(6), dma(6),
-            dma(5, 9), dma(5, 9), dma(5, 17), dma(5, 17),
+            dma(5, 20), dma(5, 20), dma(5, 20), dma(5, 20),
             dma(2, 7), dma(2, 7), dma(2, 7), dma(2, 7),
             dma(2, 4), dma(2, 4),
         ],

time: 117 us -> 116 us (level)
  Pallas kernels: 117 us -> 115 us
    pallas_call x1, Pallas kernels: 111 us -> 109 us  [shards(): pl.pallas_call(cycle, out_shape=(jax.ShapeDtypeStruct((row_tile, AUX), BF...]
where the time goes in v6:
time: 116 us; the launch traced here: 115 us
  Pallas kernels  115 us (99%)
    pallas_call x1, Pallas kernels, shards(): pl.pallas_call(cycle, out_shape=(jax.ShapeDtypeStruct((row_tile, AUX), BF...  109 us
    pallas_call x1, Pallas kernels, shards(): pl.pallas_call(finish, out_shape=jax.ShapeDtypeStruct((row_tile, col_tile...  5.71 us

profile of v6, /device:TPU:1, one launch (start us, length us, event | category | flops | bytes accessed | tf_op | source)
XLA Modules:
  0.0 115.3 jit_solution(2224765680493377162)
XLA Ops:
  0.0 109.4 %cycle.1 = (bf16[1024,768]{1,0:T(8,128)(2,1)S(1)}, bf16[2048,768]{1,0:T(8,128)(2,1)S(1)}, f32[1024,128]{1,0:T(8,128)S(1)}, f32[1,2048]{1,0:T(1,128)S(1)}) custom-call(f32[1024,2048]{1,0:T(8,128)} %amp.1, bf16[128,768]{1,0:T(8,128)(2,1)} %own_hbm.1, f32[128,128]{1,0:T(8,128)} %bitcast.1), custom_call_target="tpu_custom_call" | custom-call | tf_op jit(solution)/shard_map/cycle/pallas_call | solution.py:594
  109.4 5.7 %finish.1 = f32[1024,2048]{1,0:T(8,128)} custom-call(bf16[1024,768]{1,0:T(8,128)(2,1)S(1)} %get-tuple-element.9.dr, bf16[2048,768]{1,0:T(8,128)(2,1)S(1)} %get-tuple-element.10.dc, f32[1024,128]{1,0:T(8,128)S(1)} %get-tuple-element.11.e_row, f32[1,2048]{1,0:T(1,128)S(1)} %get-tuple-element.12.e_col), custom_call_target="tpu_custom_call" | custom-call | tf_op jit(solution)/shard_map/finish/pallas_call | solution.py:632

commit v7 on v6

--- a/solution.py
+++ b/solution.py
@@ -204,19 +204,21 @@
 
 
 def finish(dr, dc, e_row, e_col, out, stage, sem):
-    def put(i):
-        return pltpu.make_async_copy(stage.at[i % 2], out.at[pl.ds(i * 256, 256), :], sem.at[i % 2])
+    def put(i, j):
+        part = out.at[pl.ds(i * 256, 256), pl.ds(j * 512, 512)]
+        return pltpu.make_async_copy(stage.at[i % 2, j], part, sem.at[i % 2, j])
 
     for i in range(4):
-        if i >= 2:
-            put(i - 2).wait()
+        rows = slice(i * 256, (i + 1) * 256)
         for j in range(4):
             cols = slice(j * 512, (j + 1) * 512)
-            rows = slice(i * 256, (i + 1) * 256)
-            stage[i % 2, :, cols] = tile(dr[rows, :], dc[cols, :], e_row[rows, :], e_col[:, cols])
-        put(i).start()
-    put(2).wait()
-    put(3).wait()
+            if i >= 2:
+                put(i - 2, j).wait()
+            stage[i % 2, j] = tile(dr[rows, :], dc[cols, :], e_row[rows, :], e_col[:, cols])
+            put(i, j).start()
+    for i in (2, 3):
+        for j in range(4):
+            put(i, j).wait()
 
 
 def cycle(
@@ -463,14 +465,14 @@
         hx = [
             Gather(
                 line_x, dr, k, agx_s.at[1 + 2 * it + k], agx_r.at[1 + 2 * it + k],
-                relay_own=True, relay_pair=k == 0,
+                relay_own=True, relay_pair=True,
             )
             for k in range(2)
         ]
         hy = [
             Gather(
                 line_y, dc, k, agy_s.at[1 + 2 * it + k], agy_r.at[1 + 2 * it + k], half_c, other_c,
-                relay_own=True, relay_pair=k == 1,
+                relay_own=True, relay_pair=True,
             )
             for k in range(2)
         ]
@@ -634,7 +636,7 @@
         out_shape=jax.ShapeDtypeStruct((row_tile, col_tile), F32),
         in_specs=[vmem, vmem, vmem, vmem],
         out_specs=pl.BlockSpec(memory_space=pl.ANY),
-        scratch_shapes=[pltpu.VMEM((2, 256, col_tile), F32), dma(2)],
+        scratch_shapes=[pltpu.VMEM((2, 4, 256, 512), F32), dma(2, 4)],
         compiler_params=pltpu.CompilerParams(vmem_limit_bytes=20 * 1024 * 1024),
         name="finish",
     )(dr, dc, e_row, e_col)

time: 116 us -> 115 us (level)
  no operation moved by 1% of the time
where the time goes in v7:
time: 115 us
  Pallas kernels  114 us (99%)
    pallas_call x1, Pallas kernels, shards(): pl.pallas_call(cycle, out_shape=(jax.ShapeDtypeStruct((row_tile, AUX), BF...  109 us
    pallas_call x1, Pallas kernels, shards(): pl.pallas_call(finish, out_shape=jax.ShapeDtypeStruct((row_tile, col_tile...  5.93 us

profile of v7, /device:TPU:1, one launch (start us, length us, event | category | flops | bytes accessed | tf_op | source)
XLA Modules:
  0.0 114.7 jit_solution(3888862412972177285)
XLA Ops:
  0.0 108.6 %cycle.1 = (bf16[1024,768]{1,0:T(8,128)(2,1)S(1)}, bf16[2048,768]{1,0:T(8,128)(2,1)S(1)}, f32[1024,128]{1,0:T(8,128)S(1)}, f32[1,2048]{1,0:T(1,128)S(1)}) custom-call(f32[1024,2048]{1,0:T(8,128)} %amp.1, bf16[128,768]{1,0:T(8,128)(2,1)} %own_hbm.1, f32[128,128]{1,0:T(8,128)} %bitcast.1), custom_call_target="tpu_custom_call" | custom-call | tf_op jit(solution)/shard_map/cycle/pallas_call | solution.py:596
  108.6 5.9 %finish.1 = f32[1024,2048]{1,0:T(8,128)} custom-call(bf16[1024,768]{1,0:T(8,128)(2,1)S(1)} %get-tuple-element.9.dr, bf16[2048,768]{1,0:T(8,128)(2,1)S(1)} %get-tuple-element.10.dc, f32[1024,128]{1,0:T(8,128)S(1)} %get-tuple-element.11.e_row, f32[1,2048]{1,0:T(1,128)S(1)} %get-tuple-element.12.e_col), custom_call_target="tpu_custom_call" | custom-call | tf_op jit(solution)/shard_map/finish/pallas_call | solution.py:634

commit v8 on v7

--- a/solution.py
+++ b/solution.py
@@ -523,10 +523,10 @@
         hy[0].start()
         hy[1].near()
         hx[0].near()
+        hy[0].pair()
+        hx[1].pair()
         hy[1].near_pair()
         hx[0].near_pair()
-        hy[0].pair()
-        hx[1].pair()
         hy[1].far()
         hx[0].far()
         hy[0].near()

time: 115 us -> 119 us (1.035)
  Pallas kernels: 114 us -> 118 us
    pallas_call x1, Pallas kernels: 109 us -> 112 us  [shards(): pl.pallas_call(cycle, out_shape=(jax.ShapeDtypeStruct((row_tile, AUX), BF...]
where the time goes in v8:
time: 119 us; the launch traced here: 118 us
  Pallas kernels  118 us (99%)
    pallas_call x1, Pallas kernels, shards(): pl.pallas_call(cycle, out_shape=(jax.ShapeDtypeStruct((row_tile, AUX), BF...  112 us
    pallas_call x1, Pallas kernels, shards(): pl.pallas_call(finish, out_shape=jax.ShapeDtypeStruct((row_tile, col_tile...  5.93 us

profile of v8, /device:TPU:1, one launch (start us, length us, event | category | flops | bytes accessed | tf_op | source)
XLA Modules:
  0.0 117.9 jit_solution(5506897129714061120)
XLA Ops:
  0.0 111.8 %cycle.1 = (bf16[1024,768]{1,0:T(8,128)(2,1)S(1)}, bf16[2048,768]{1,0:T(8,128)(2,1)S(1)}, f32[1024,128]{1,0:T(8,128)S(1)}, f32[1,2048]{1,0:T(1,128)S(1)}) custom-call(f32[1024,2048]{1,0:T(8,128)} %amp.1, bf16[128,768]{1,0:T(8,128)(2,1)} %own_hbm.1, f32[128,128]{1,0:T(8,128)} %bitcast.1), custom_call_target="tpu_custom_call" | custom-call | tf_op jit(solution)/shard_map/cycle/pallas_call | solution.py:596
  111.8 5.9 %finish.1 = f32[1024,2048]{1,0:T(8,128)} custom-call(bf16[1024,768]{1,0:T(8,128)(2,1)S(1)} %get-tuple-element.9.dr, bf16[2048,768]{1,0:T(8,128)(2,1)S(1)} %get-tuple-element.10.dc, f32[1024,128]{1,0:T(8,128)S(1)} %get-tuple-element.11.e_row, f32[1,2048]{1,0:T(1,128)S(1)} %get-tuple-element.12.e_col), custom_call_target="tpu_custom_call" | custom-call | tf_op jit(solution)/shard_map/finish/pallas_call | solution.py:634
